TPU v7x, 256 devices: a whole 4x4x8 slice. The times are simulated.
256 devices in a mesh: wall: 16 (over y, x), stream: 16 (over z, core).
Axes of the slice: x: 4, y: 4, z: 8, core: 2. Of those that a mesh axis runs over, the one named last changes fastest.
Arguments:
- residual_rhs: float32 [128, 16, 2048], P('wall', None, 'stream'), may hold values from -6 to 6
- pivot_inverse: bfloat16 [128, 16, 16, 2048], P('wall', None, None, 'stream'), may hold values from -0.3125 to 0.3125
- lower_factor: bfloat16 [128, 16, 16, 2048], P('wall', None, None, 'stream'), may hold values from -1 to 1
- upper_factor: bfloat16 [128, 16, 16, 2048], P('wall', None, None, 'stream'), may hold values from -1 to 1
- west_jacobian: bfloat16 [128, 16, 16, 2048], P('wall', None, None, 'stream'), may hold values from -0.1875 to 0.1875
- east_jacobian: bfloat16 [128, 16, 16, 2048], P('wall', None, None, 'stream'), may hold values from -0.1875 to 0.1875
- species_mask: int32 [16, 16], replicated, may hold values 0 or 1
- cell_codes: int32 [128, 2048], P('wall', 'stream'), may hold values from 0 to 3
Outputs:
- update: float32 [128, 16, 2048], P('wall', None, 'stream')
All inputs are finite; a program needn't handle non-finite values.
Results may differ from a plain program's by a relative error of at most 0.0003.
Values sent between devices are 32-bit elements; how exact they have to be, the bound alone decides.
A program may use at most 64 MiB of HBM per device.

v0:
```python
import math

import jax
import jax.numpy as jnp
from jax import lax
from jax.sharding import PartitionSpec as P

SWEEPS = 3


def joined_along(parts, dim):
    shape = list(parts.shape[1:])
    shape[dim] *= parts.shape[0]
    return jnp.moveaxis(parts, 0, dim).reshape(shape)


def sent_to_all(x, axis):
    copies = jnp.broadcast_to(x, (lax.axis_size(axis), *x.shape))
    return lax.all_to_all(copies, axis, split_axis=0, concat_axis=0, tiled=True)


def collect(x, axis, dim):
    return joined_along(sent_to_all(x, axis), dim)


def in_one_piece(arrays, axis, dim, along):
    widths = [math.prod(a.shape[along:]) for a in arrays]
    both = jnp.concatenate(
        [a.reshape(*a.shape[:along], w) for a, w in zip(arrays, widths)], axis=along
    )
    out = collect(both, axis, dim)
    parts = jnp.split(out, [sum(widths[:k]) for k in range(1, len(widths))], axis=along)
    return tuple((b.reshape(*out.shape[:along], *a.shape[along:]) for a, b in zip(arrays, parts)))


def extended(block, sides, width):
    for axis, dim in sides:
        count = lax.axis_size(axis)
        forward = [(i, i + 1) for i in range(count - 1)]
        backward = [(target, source) for source, target in forward]
        low = lax.ppermute(
            lax.slice_in_dim(block, block.shape[dim] - width, None, axis=dim), axis, forward
        )
        high = lax.ppermute(lax.slice_in_dim(block, 0, width, axis=dim), axis, backward)
        block = jnp.concatenate([low, block, high], axis=dim)
    return block


def multiply_cells(blocks, vectors):
    summed = blocks[..., :, 0, :].astype(jnp.float32) * vectors[..., 0:1, :]
    for column in range(1, blocks.shape[-2]):
        summed = (
            summed
            + blocks[..., :, column, :].astype(jnp.float32) * vectors[..., column : column + 1, :]
        )
    return summed


def map_times(chain_map, vectors):
    return jnp.einsum("cks,ks->cs", chain_map, vectors, precision=lax.Precision.HIGHEST)


def local_map(factor, source, reverse):
    width = source.shape[1]
    lanes = source.shape[2]
    identity_map = jnp.broadcast_to(
        jnp.eye(width, dtype=jnp.float32)[:, :, None], (width, width, lanes)
    )

    def local_advance(running, inputs):
        chain_map, current = running
        factor_cell, source_cell = inputs
        current = source_cell + multiply_cells(factor_cell, current)
        chain_map = jnp.einsum(
            "cks,kms->cms",
            factor_cell.astype(jnp.float32),
            chain_map,
            precision=lax.Precision.HIGHEST,
        )
        return ((chain_map, current), None)

    start = (identity_map, jnp.zeros((width, lanes), jnp.float32))
    (chain_map, current), _ = lax.scan(local_advance, start, (factor, source), reverse=reverse)
    return (chain_map, current)


def run_chain(factor, source, inflow, reverse):

    def run_advance(current, inputs):
        factor_cell, source_cell = inputs
        current = source_cell + multiply_cells(factor_cell, current)
        return (current, current)

    _, result = lax.scan(run_advance, inflow, (factor, source), reverse=reverse)
    return result


def inflow_for(chain_map, current, reverse):
    width = current.shape[0]
    lanes = current.shape[1]
    zero_vec = jnp.zeros((width, lanes), jnp.float32)
    if reverse:
        every_p, every_q = in_one_piece((chain_map[None], current[None]), "wall", 0, 2)
    else:
        every_p, every_q = in_one_piece((chain_map[None], current[None]), "wall", 0, 2)
    wall_devices = every_p.shape[0]
    own_index = lax.axis_index("wall")

    def absorb(turn, gathered_in):
        if reverse:
            source_dev = wall_devices - 1 - turn
            include = source_dev > own_index
        else:
            source_dev = turn
            include = source_dev < own_index
        piece_p = lax.dynamic_index_in_dim(every_p, source_dev, 0, keepdims=False)
        piece_q = lax.dynamic_index_in_dim(every_q, source_dev, 0, keepdims=False)
        moved = map_times(piece_p, gathered_in) + piece_q
        return jnp.where(include, moved, gathered_in)

    return lax.fori_loop(0, wall_devices, absorb, zero_vec)


def on_device(
    residual_rhs,
    pivot_inverse,
    lower_factor,
    upper_factor,
    west_jacobian,
    east_jacobian,
    species_mask,
    cell_codes,
):
    mask_bf = species_mask.astype(jnp.bfloat16)[None, :, :, None]
    west_masked = west_jacobian * mask_bf
    east_masked = east_jacobian * mask_bf
    west_on = ((cell_codes == 0) | (cell_codes == 1)).astype(jnp.float32)[:, None, :]
    east_on = ((cell_codes == 0) | (cell_codes == 2)).astype(jnp.float32)[:, None, :]
    update = jnp.zeros(residual_rhs.shape, jnp.float32)
    for sweep_index in range(SWEEPS):
        source = residual_rhs
        if sweep_index > 0:
            padded = extended(update, (("stream", 2),), 1)
            source = source - west_on * multiply_cells(west_masked, padded[:, :, :-2])
            source = source - east_on * multiply_cells(east_masked, padded[:, :, 2:])
        forward = multiply_cells(pivot_inverse, source)
        chain_map, current = local_map(lower_factor, forward, False)
        inflow = inflow_for(chain_map, current, False)
        forward_lines = run_chain(lower_factor, forward, inflow, False)
        chain_map, current = local_map(upper_factor, forward_lines, True)
        inflow = inflow_for(chain_map, current, True)
        update = run_chain(upper_factor, forward_lines, inflow, True)
    return update


def solution(mesh):
    return jax.shard_map(
        on_device,
        mesh=mesh,
        in_specs=(
            P("wall", None, "stream"),
            P("wall", None, None, "stream"),
            P("wall", None, None, "stream"),
            P("wall", None, None, "stream"),
            P("wall", None, None, "stream"),
            P("wall", None, None, "stream"),
            P(),
            P("wall", "stream"),
        ),
        out_specs=P("wall", None, "stream"),
        check_vma=False,
    )
```

profile of v0, /device:TPU:8, one launch (start us, length us, event | category | flops | bytes accessed | tf_op | source)
XLA Modules:
  0.0 484.5 jit_solution(17104105745630097357)
XLA Ops:
  0.0 4.1 fusion.613
  5.1 10.1 %while.270 = (s32[]{:T(128)}, f32[16,16,128]{1,0,2:T(8,128)S(1)}, f32[16,128]{1,0:T(8,128)S(1)}, bf16[8,16,16,128]{3,1,2,0:T(8,128)(2,1)S(1)}, f32[8,16,128]{2,1,0:T(8,128)S(1)}, /*index=5*/s32[]{:T(128)}, s32[]{:T(128)}) while((s32[]{:T(128)}, f32[16,16,128]{1,0,2:T(8,128)S(1)}, f32[16,128]{1,0:T(8,128)S(1)}, ...), condition=%wide.region_1.2_spmd.clone, body=%wide.region_0.1_spmd.clone.sunk | while | flops 6391811 | bytes 974943 | solution.py:83
  17.2 7.4 %all-to-all-start = ((f32[16,1,16,2176]{3,2,1,0:T(8,128)}), f32[16,1,16,2176]{3,2,1,0:T(8,128)S(1)}, u32[]{:S(2)}, u32[]{:S(2)}) async-start(f32[16,1,16,2176]{3,2,1,0:T(8,128)} %broadcast_in_dim.84), calls=%async_computation | async-start | bytes 4456448 | tf_op jit(solution)/shard_map/all_to_all | solution.py:19
  25.8 31.1 %all-to-all-done = f32[16,1,16,2176]{3,2,1,0:T(8,128)S(1)} async-done(((f32[16,1,16,2176]{3,2,1,0:T(8,128)}), f32[16,1,16,2176]{3,2,1,0:T(8,128)S(1)}, u32[]{:S(2)}, u32[]{:S(2)}) %all-to-all-start) | async-done | bytes 2228256 | tf_op jit(solution)/shard_map/all_to_all | solution.py:19
  58.2 12.0 %while.271 = (s32[]{:T(128)}, f32[16,128]{1,0:T(8,128)S(1)}, s32[]{:T(128)}, f32[16,16,16,128]{3,2,1,0:T(8,128)S(1)}, f32[16,16,128]{2,1,0:T(8,128)}, /*index=5*/s32[]{:T(128)}, s32[]{:T(128)}) while((s32[]{:T(128)}, f32[16,128]{1,0:T(8,128)S(1)}, s32[]{:T(128)}, f32[16,16,16,128]{3,2,1,0:T(8,128)S(1)}, f32[16,16,128]{2,1,0:T(8,128)}, ...), condition=%wide.region_3.4_spmd.clone, body=%wide.region_2.3_spmd.clone.sunk | while | flops 71684 | bytes 196714 | solution.py:121
  70.3 12.1 %while.264 = (s32[]{:T(128)}, f32[16,128]{1,0:T(8,128)S(1)}, f32[8,16,128]{2,1,0:T(8,128)S(1)}, f32[8,16,128]{2,1,0:T(8,128)}, bf16[8,16,16,128]{3,1,2,0:T(8,128)(2,1)S(1)}, /*index=5*/s32[]{:T(128)}) while((s32[]{:T(128)}, f32[16,128]{1,0:T(8,128)S(1)}, f32[8,16,128]{2,1,0:T(8,128)S(1)}, f32[8,16,128]{2,1,0:T(8,128)}, ...), condition=%wide.region_5.6_spmd, body=%wide.region_4.5_spmd.sunk | while | flops 196610 | bytes 327761 | solution.py:94
  82.5 10.1 %while.272 = (s32[]{:T(128)}, f32[16,16,128]{1,0,2:T(8,128)S(1)}, f32[16,128]{1,0:T(8,128)S(1)}, bf16[8,16,16,128]{3,1,2,0:T(8,128)(2,1)S(1)}, f32[8,16,128]{2,1...) while((s32[]{:T(128)}, f32[16,16,128]{1,0,2:T(8,128)S(1)}, f32[16,128]{1,0:T(8,128)S(1)}, ...), condition=%wide.region_7.8_spmd.clone, body=%wide.region_6.7_spmd.clone.sunk | while | flops 6391812 | bytes 974963 | solution.py:83
  94.6 5.8 %all-to-all-start.1 = ((f32[16,1,16,2176]{3,2,1,0:T(8,128)}), f32[16,1,16,2176]{3,2,1,0:T(8,128)}, u32[]{:S(2)}, u32[]{:S(2)}) async-start(f32[16,1,16,2176]{3,2,1,0:T(8,128)} %broadcast_in_dim.86), calls=%async_computation.1 | async-start | bytes 4456448 | tf_op jit(solution)/shard_map/all_to_all | solution.py:19
  101.4 1.7 fusion.612
  103.3 27.4 %all-to-all-done.1 = f32[16,1,16,2176]{3,2,1,0:T(8,128)} async-done(((f32[16,1,16,2176]{3,2,1,0:T(8,128)}), f32[16,1,16,2176]{3,2,1,0:T(8,128)}, u32[]{:S(2)}, u32[]{:S(2)}) %all-to-all-start.1) | async-done | bytes 2228256 | tf_op jit(solution)/shard_map/all_to_all | solution.py:19
  130.7 1.7 split.50
  135.0 16.0 %while.273 = (s32[]{:T(128)}, f32[16,128]{1,0:T(8,128)S(1)}, s32[]{:T(128)}, f32[16,16,16,128]{3,2,1,0:T(8,128)}, f32[16,16,128]{2,1,0:T(8,128)S(1)}, /*index=5*/s32[]{:T(128)}, s32[]{:T(128)}, s32[]{:T(128)}, s32[]{:T(128)}) while((s32[]{:T(128)}, f32[16,128]{1,0:T(8,128)S(1)}, s32[]{:T(128)}, f32[16,16,16,128]{3,2,1,0:T(8,128)}, ...), condition=%wide.region_9.10_spmd.clone, body=%wide.region_8.9_spmd.clone.sunk | while | flops 71688 | bytes 196776 | solution.py:121
  151.1 18.0 %while.265 = (s32[]{:T(128)}, f32[16,128]{1,0:T(8,128)S(1)}, f32[8,16,128]{2,1,0:T(8,128)S(1)}, f32[8,16,128]{2,1,0:T(8,128)}, bf16[8,16,16,128]{3,1,2,0:T(8,128)(2,1)S(1)}, /*index=5*/s32[]{:T(128)}, s32[]{:T(128)}) while((s32[]{:T(128)}, f32[16,128]{1,0:T(8,128)S(1)}, f32[8,16,128]{2,1,0:T(8,128)S(1)}, f32[8,16,128]{2,1,0:T(8,128)}, ...), condition=%wide.region_11.12_spmd, body=%wide.region_10.11_spmd.sunk | while | flops 196611 | bytes 327781 | solution.py:94
  170.5 3.2 collective-permute-start
  176.9 10.1 %while.274 = (s32[]{:T(128)}, f32[16,16,128]{1,0,2:T(8,128)S(1)}, f32[16,128]{1,0:T(8,128)S(1)}, bf16[8,16,16,128]{3,1,2,0:T(8,128)(2,1)S(1)}, f32[8,16,128]{2,1,0:T(8,128)S(1)}, /*index=5*/s32[]{:T(128)}, s32[]{:T(128)}) while((s32[]{:T(128)}, f32[16,16,128]{1,0,2:T(8,128)S(1)}, f32[16,128]{1,0:T(8,128)S(1)}, ...), condition=%wide.region_13.14_spmd.clone, body=%wide.region_12.13_spmd.clone.sunk | while | flops 6391811 | bytes 974943 | solution.py:83
  189.0 5.2 %all-to-all-start.2 = ((f32[16,1,16,2176]{3,2,1,0:T(8,128)}), f32[16,1,16,2176]{3,2,1,0:T(8,128)S(1)}, u32[]{:S(2)}, u32[]{:S(2)}) async-start(f32[16,1,16,2176]{3,2,1,0:T(8,128)} %broadcast_in_dim.88), calls=%async_computation.2 | async-start | bytes 4456448 | tf_op jit(solution)/shard_map/all_to_all | solution.py:19
  194.2 33.6 %all-to-all-done.2 = f32[16,1,16,2176]{3,2,1,0:T(8,128)S(1)} async-done(((f32[16,1,16,2176]{3,2,1,0:T(8,128)}), f32[16,1,16,2176]{3,2,1,0:T(8,128)S(1)}, u32[]{:S(2)}, u32[]{:S(2)}) %all-to-all-start.2) | async-done | bytes 2228256 | tf_op jit(solution)/shard_map/all_to_all | solution.py:19
  229.1 12.0 %while.275 = (s32[]{:T(128)}, f32[16,128]{1,0:T(8,128)S(1)}, s32[]{:T(128)}, f32[16,16,16,128]{3,2,1,0:T(8,128)S(1)}, f32[16,16,128]{2,1,0:T(8,128)}, /*index=5*/s32[]{:T(128)}, s32[]{:T(128)}) while((s32[]{:T(128)}, f32[16,128]{1,0:T(8,128)S(1)}, s32[]{:T(128)}, f32[16,16,16,128]{3,2,1,0:T(8,128)S(1)}, ...), condition=%wide.region_15.16_spmd.clone, body=%wide.region_14.15_spmd.clone.sunk | while | flops 71684 | bytes 196714 | solution.py:121
  241.2 12.1 %while.266 = (s32[]{:T(128)}, f32[16,128]{1,0:T(8,128)S(1)}, f32[8,16,128]{2,1,0:T(8,128)S(1)}, f32[8,16,128]{2,1,0:T(8,128)}, bf16[8,16,16,128]{3,1,2,0:T(8,128)(2,1)S(1)}, /*index=5*/s32[]{:T(128)}) while((s32[]{:T(128)}, f32[16,128]{1,0:T(8,128)S(1)}, f32[8,16,128]{2,1,0:T(8,128)S(1)}, f32[8,16,128]{2,1,0:T(8,128)}, ...), condition=%wide.region_17.18_spmd, body=%wide.region_16.17_spmd.sunk | while | flops 196610 | bytes 327761 | solution.py:94
  253.3 10.1 %while.276 = (s32[]{:T(128)}, f32[16,16,128]{1,0,2:T(8,128)S(1)}, f32[16,128]{1,0:T(8,128)S(1)}, bf16[8,16,16,128]{3,1,2,0:T(8,128)(2,1)S(1)}, f32[8,16,128]{2,1...) while((s32[]{:T(128)}, f32[16,16,128]{1,0,2:T(8,128)S(1)}, f32[16,128]{1,0:T(8,128)S(1)}, ...), condition=%wide.region_19.20_spmd.clone, body=%wide.region_18.19_spmd.clone.sunk | while | flops 6391812 | bytes 974963 | solution.py:83
  265.5 5.5 %all-to-all-start.3 = ((f32[16,1,16,2176]{3,2,1,0:T(8,128)}), f32[16,1,16,2176]{3,2,1,0:T(8,128)S(1)}, u32[]{:S(2)}, u32[]{:S(2)}) async-start(f32[16,1,16,2176]{3,2,1,0:T(8,128)} %broadcast_in_dim.90), calls=%async_computation.3 | async-start | bytes 4456448 | tf_op jit(solution)/shard_map/all_to_all | solution.py:19
  271.0 35.1 %all-to-all-done.3 = f32[16,1,16,2176]{3,2,1,0:T(8,128)S(1)} async-done(((f32[16,1,16,2176]{3,2,1,0:T(8,128)}), f32[16,1,16,2176]{3,2,1,0:T(8,128)S(1)}, u32[]{:S(2)}, u32[]{:S(2)}) %all-to-all-start.3) | async-done | bytes 2228256 | tf_op jit(solution)/shard_map/all_to_all | solution.py:19
  308.8 26.5 %while.277 = (s32[]{:T(128)}, f32[16,128]{1,0:T(8,128)S(1)}, s32[]{:T(128)}, f32[16,16,16,128]{3,2,1,0:T(8,128)}, f32[16,16,128]{2,1,0:T(8,128)}, /*index=5*/s32[]{:T(128)}, s32[]{:T(128)}, s32[]{:T(128)}, s32[]{:T(128)}) while((s32[]{:T(128)}, f32[16,128]{1,0:T(8,128)S(1)}, s32[]{:T(128)}, f32[16,16,16,128]{3,2,1,0:T(8,128)}, ...), condition=%wide.region_21.22_spmd.clone, body=%wide.region_20.21_spmd.clone.sunk | while | flops 71688 | bytes 196776 | solution.py:121
  335.4 18.3 %while.267 = (s32[]{:T(128)}, f32[16,128]{1,0:T(8,128)S(1)}, f32[8,16,128]{2,1,0:T(8,128)S(1)}, f32[8,16,128]{2,1,0:T(8,128)}, bf16[8,16,16,128]{3,1,2,0:T(8,128)(2,1)S(1)}, /*index=5*/s32[]{:T(128)}, s32[]{:T(128)}) while((s32[]{:T(128)}, f32[16,128]{1,0:T(8,128)S(1)}, f32[8,16,128]{2,1,0:T(8,128)S(1)}, f32[8,16,128]{2,1,0:T(8,128)}, ...), condition=%wide.region_23.24_spmd, body=%wide.region_22.23_spmd.sunk | while | flops 196611 | bytes 327781 | solution.py:94
  355.2 3.0 collective-permute-start.2
  361.3 10.1 %while.278 = (s32[]{:T(128)}, f32[16,16,128]{1,0,2:T(8,128)S(1)}, f32[16,128]{1,0:T(8,128)S(1)}, bf16[8,16,16,128]{3,1,2,0:T(8,128)(2,1)S(1)}, f32[8,16,128]{2,1,0:T(8,128)S(1)}, /*index=5*/s32[]{:T(128)}, s32[]{:T(128)}) while((s32[]{:T(128)}, f32[16,16,128]{1,0,2:T(8,128)S(1)}, f32[16,128]{1,0:T(8,128)S(1)}, ...), condition=%wide.region_25.26_spmd.clone, body=%wide.region_24.25_spmd.clone.sunk | while | flops 6391811 | bytes 974943 | solution.py:83
  373.4 5.8 %all-to-all-start.4 = ((f32[16,1,16,2176]{3,2,1,0:T(8,128)}), f32[16,1,16,2176]{3,2,1,0:T(8,128)S(1)}, u32[]{:S(2)}, u32[]{:S(2)}) async-start(f32[16,1,16,2176]{3,2,1,0:T(8,128)} %broadcast_in_dim.92), calls=%async_computation.4 | async-start | bytes 4456448 | tf_op jit(solution)/shard_map/all_to_all | solution.py:19
  379.2 35.0 %all-to-all-done.4 = f32[16,1,16,2176]{3,2,1,0:T(8,128)S(1)} async-done(((f32[16,1,16,2176]{3,2,1,0:T(8,128)}), f32[16,1,16,2176]{3,2,1,0:T(8,128)S(1)}, u32[]{:S(2)}, u32[]{:S(2)}) %all-to-all-start.4) | async-done | bytes 2228256 | tf_op jit(solution)/shard_map/all_to_all | solution.py:19
  416.4 12.1 %while.268 = (s32[]{:T(128)}, f32[16,128]{1,0:T(8,128)S(1)}, f32[8,16,128]{2,1,0:T(8,128)S(1)}, f32[8,16,128]{2,1,0:T(8,128)}, bf16[8,16,16,128]{3,1,2,0:T(8,128)(2,1)S(1)}, /*index=5*/s32[]{:T(128)}) while((s32[]{:T(128)}, f32[16,128]{1,0:T(8,128)S(1)}, f32[8,16,128]{2,1,0:T(8,128)S(1)}, f32[8,16,128]{2,1,0:T(8,128)}, ...), condition=%wide.region_29.30_spmd, body=%wide.region_28.29_spmd.sunk | while | flops 196610 | bytes 327761 | solution.py:94
  428.6 10.1 %while.280 = (s32[]{:T(128)}, f32[16,16,128]{1,0,2:T(8,128)S(1)}, f32[16,128]{1,0:T(8,128)S(1)}, bf16[8,16,16,128]{3,1,2,0:T(8,128)(2,1)S(1)}, f32[8,16,128]{2,1...) while((s32[]{:T(128)}, f32[16,16,128]{1,0,2:T(8,128)S(1)}, f32[16,128]{1,0:T(8,128)S(1)}, ...), condition=%wide.region_31.32_spmd.clone, body=%wide.region_30.31_spmd.clone.sunk | while | flops 6391812 | bytes 974963 | solution.py:83
  440.7 5.3 %all-to-all-start.5 = ((f32[16,1,16,2176]{3,2,1,0:T(8,128)}), f32[16,1,16,2176]{3,2,1,0:T(8,128)S(1)}, u32[]{:S(2)}, u32[]{:S(2)}) async-start(f32[16,1,16,2176]{3,2,1,0:T(8,128)} %broadcast_in_dim.94), calls=%async_computation.5 | async-start | bytes 4456448 | tf_op jit(solution)/shard_map/all_to_all | solution.py:19
  446.0 34.5 %all-to-all-done.5 = f32[16,1,16,2176]{3,2,1,0:T(8,128)S(1)} async-done(((f32[16,1,16,2176]{3,2,1,0:T(8,128)}), f32[16,1,16,2176]{3,2,1,0:T(8,128)S(1)}, u32[]{:S(2)}, u32[]{:S(2)}) %all-to-all-start.5) | async-done | bytes 2228256 | tf_op jit(solution)/shard_map/all_to_all | solution.py:19
  (1078 shorter events, 234.2 us)
Async XLA Ops:
  17.2 39.7 %all-to-all-start = ((f32[16,1,16,2176]{3,2,1,0:T(8,128)}), f32[16,1,16,2176]{3,2,1,0:T(8,128)S(1)}, u32[]{:S(2)}, u32[]{:S(2)}) async-start(f32[16,1,16,2176]{3,2,1,0:T(8,128)} %broadcast_in_dim.84), calls=%async_computation | async-start | bytes 4456448 | tf_op jit(solution)/shard_map/all_to_all | solution.py:19
  94.6 36.0 %all-to-all-start.1 = ((f32[16,1,16,2176]{3,2,1,0:T(8,128)}), f32[16,1,16,2176]{3,2,1,0:T(8,128)}, u32[]{:S(2)}, u32[]{:S(2)}) async-start(f32[16,1,16,2176]{3,2,1,0:T(8,128)} %broadcast_in_dim.86), calls=%async_computation.1 | async-start | bytes 4456448 | tf_op jit(solution)/shard_map/all_to_all | solution.py:19
  101.4 73.3 %copy-start = (bf16[8,16,16,128]{3,1,0,2:T(8,128)(2,1)}, bf16[8,16,16,128]{3,1,0,2:T(8,128)(2,1)S(1)}, u32[]{:S(2)}) copy-start(bf16[8,16,16,128]{3,1,0,2:T(8,128)(2,1)S(1)} %copy_multiply_fusion) | copy-start | bytes 1572868
  103.2 71.5 %copy-start.38 = (bf16[8,16,1,128]{3,2,1,0:T(2,128)(2,1)}, bf16[8,16,1,128]{3,2,1,0:T(2,128)(2,1)S(1)}, u32[]{:S(2)}) copy-start(bf16[8,16,1,128]{3,2,1,0:T(2,128)(2,1)S(1)} %get-tuple-element.3221) | copy-start | bytes 98308
  103.2 71.6 %copy-start.40 = (bf16[8,16,1,128]{3,2,1,0:T(2,128)(2,1)}, bf16[8,16,1,128]{3,2,1,0:T(2,128)(2,1)S(1)}, u32[]{:S(2)}) copy-start(bf16[8,16,1,128]{3,2,1,0:T(2,128)(2,1)S(1)} %get-tuple-element.3222) | copy-start | bytes 98308
  103.2 71.6 %copy-start.42 = (bf16[8,16,1,128]{3,2,1,0:T(2,128)(2,1)}, bf16[8,16,1,128]{3,2,1,0:T(2,128)(2,1)S(1)}, u32[]{:S(2)}) copy-start(bf16[8,16,1,128]{3,2,1,0:T(2,128)(2,1)S(1)} %get-tuple-element.3223) | copy-start | bytes 98308
  103.2 71.6 %copy-start.44 = (bf16[8,16,1,128]{3,2,1,0:T(2,128)(2,1)}, bf16[8,16,1,128]{3,2,1,0:T(2,128)(2,1)S(1)}, u32[]{:S(2)}) copy-start(bf16[8,16,1,128]{3,2,1,0:T(2,128)(2,1)S(1)} %get-tuple-element.3224) | copy-start | bytes 98308
  103.2 71.6 %copy-start.46 = (bf16[8,16,1,128]{3,2,1,0:T(2,128)(2,1)}, bf16[8,16,1,128]{3,2,1,0:T(2,128)(2,1)S(1)}, u32[]{:S(2)}) copy-start(bf16[8,16,1,128]{3,2,1,0:T(2,128)(2,1)S(1)} %get-tuple-element.3225) | copy-start | bytes 98308
  103.2 71.6 %copy-start.48 = (bf16[8,16,1,128]{3,2,1,0:T(2,128)(2,1)}, bf16[8,16,1,128]{3,2,1,0:T(2,128)(2,1)S(1)}, u32[]{:S(2)}) copy-start(bf16[8,16,1,128]{3,2,1,0:T(2,128)(2,1)S(1)} %get-tuple-element.3226) | copy-start | bytes 98308
  103.2 71.6 %copy-start.50 = (bf16[8,16,1,128]{3,2,1,0:T(2,128)(2,1)}, bf16[8,16,1,128]{3,2,1,0:T(2,128)(2,1)S(1)}, u32[]{:S(2)}) copy-start(bf16[8,16,1,128]{3,2,1,0:T(2,128)(2,1)S(1)} %get-tuple-element.3227) | copy-start | bytes 98308
  103.2 71.6 %copy-start.52 = (bf16[8,16,1,128]{3,2,1,0:T(2,128)(2,1)}, bf16[8,16,1,128]{3,2,1,0:T(2,128)(2,1)S(1)}, u32[]{:S(2)}) copy-start(bf16[8,16,1,128]{3,2,1,0:T(2,128)(2,1)S(1)} %get-tuple-element.3228) | copy-start | bytes 98308
  103.2 71.6 %copy-start.54 = (bf16[8,16,1,128]{3,2,1,0:T(2,128)(2,1)}, bf16[8,16,1,128]{3,2,1,0:T(2,128)(2,1)S(1)}, u32[]{:S(2)}) copy-start(bf16[8,16,1,128]{3,2,1,0:T(2,128)(2,1)S(1)} %get-tuple-element.3229) | copy-start | bytes 98308
  103.2 71.6 %copy-start.56 = (bf16[8,16,1,128]{3,2,1,0:T(2,128)(2,1)}, bf16[8,16,1,128]{3,2,1,0:T(2,128)(2,1)S(1)}, u32[]{:S(2)}) copy-start(bf16[8,16,1,128]{3,2,1,0:T(2,128)(2,1)S(1)} %get-tuple-element.3230) | copy-start | bytes 98308
  103.2 71.6 %copy-start.58 = (bf16[8,16,1,128]{3,2,1,0:T(2,128)(2,1)}, bf16[8,16,1,128]{3,2,1,0:T(2,128)(2,1)S(1)}, u32[]{:S(2)}) copy-start(bf16[8,16,1,128]{3,2,1,0:T(2,128)(2,1)S(1)} %get-tuple-element.3231) | copy-start | bytes 98308
  103.2 71.6 %copy-start.60 = (bf16[8,16,1,128]{3,2,1,0:T(2,128)(2,1)}, bf16[8,16,1,128]{3,2,1,0:T(2,128)(2,1)S(1)}, u32[]{:S(2)}) copy-start(bf16[8,16,1,128]{3,2,1,0:T(2,128)(2,1)S(1)} %get-tuple-element.3232) | copy-start | bytes 98308
  103.3 71.6 %copy-start.62 = (bf16[8,16,1,128]{3,2,1,0:T(2,128)(2,1)}, bf16[8,16,1,128]{3,2,1,0:T(2,128)(2,1)S(1)}, u32[]{:S(2)}) copy-start(bf16[8,16,1,128]{3,2,1,0:T(2,128)(2,1)S(1)} %get-tuple-element.3233) | copy-start | bytes 98308
  169.2 4.5 collective-permute-start.1
  170.5 3.9 collective-permute-start
  189.0 38.8 %all-to-all-start.2 = ((f32[16,1,16,2176]{3,2,1,0:T(8,128)}), f32[16,1,16,2176]{3,2,1,0:T(8,128)S(1)}, u32[]{:S(2)}, u32[]{:S(2)}) async-start(f32[16,1,16,2176]{3,2,1,0:T(8,128)} %broadcast_in_dim.88), calls=%async_computation.2 | async-start | bytes 4456448 | tf_op jit(solution)/shard_map/all_to_all | solution.py:19
  265.5 40.6 %all-to-all-start.3 = ((f32[16,1,16,2176]{3,2,1,0:T(8,128)}), f32[16,1,16,2176]{3,2,1,0:T(8,128)S(1)}, u32[]{:S(2)}, u32[]{:S(2)}) async-start(f32[16,1,16,2176]{3,2,1,0:T(8,128)} %broadcast_in_dim.90), calls=%async_computation.3 | async-start | bytes 4456448 | tf_op jit(solution)/shard_map/all_to_all | solution.py:19
  308.7 50.7 %copy-start.45 = (bf16[8,16,1,128]{3,2,1,0:T(2,128)(2,1)S(1)}, bf16[8,16,1,128]{3,2,1,0:T(2,128)(2,1)}, u32[]{:S(2)}) copy-start(bf16[8,16,1,128]{3,2,1,0:T(2,128)(2,1)} %copy-done.44) | copy-start | bytes 98308
  308.7 50.7 %copy-start.47 = (bf16[8,16,1,128]{3,2,1,0:T(2,128)(2,1)S(1)}, bf16[8,16,1,128]{3,2,1,0:T(2,128)(2,1)}, u32[]{:S(2)}) copy-start(bf16[8,16,1,128]{3,2,1,0:T(2,128)(2,1)} %copy-done.46) | copy-start | bytes 98308
  308.7 50.7 %copy-start.49 = (bf16[8,16,1,128]{3,2,1,0:T(2,128)(2,1)S(1)}, bf16[8,16,1,128]{3,2,1,0:T(2,128)(2,1)}, u32[]{:S(2)}) copy-start(bf16[8,16,1,128]{3,2,1,0:T(2,128)(2,1)} %copy-done.48) | copy-start | bytes 98308
  308.7 50.7 %copy-start.51 = (bf16[8,16,1,128]{3,2,1,0:T(2,128)(2,1)S(1)}, bf16[8,16,1,128]{3,2,1,0:T(2,128)(2,1)}, u32[]{:S(2)}) copy-start(bf16[8,16,1,128]{3,2,1,0:T(2,128)(2,1)} %copy-done.50) | copy-start | bytes 98308
  308.7 50.7 %copy-start.53 = (bf16[8,16,1,128]{3,2,1,0:T(2,128)(2,1)S(1)}, bf16[8,16,1,128]{3,2,1,0:T(2,128)(2,1)}, u32[]{:S(2)}) copy-start(bf16[8,16,1,128]{3,2,1,0:T(2,128)(2,1)} %copy-done.52) | copy-start | bytes 98308
  308.7 50.7 %copy-start.55 = (bf16[8,16,1,128]{3,2,1,0:T(2,128)(2,1)S(1)}, bf16[8,16,1,128]{3,2,1,0:T(2,128)(2,1)}, u32[]{:S(2)}) copy-start(bf16[8,16,1,128]{3,2,1,0:T(2,128)(2,1)} %copy-done.54) | copy-start | bytes 98308
  308.7 50.7 %copy-start.57 = (bf16[8,16,1,128]{3,2,1,0:T(2,128)(2,1)S(1)}, bf16[8,16,1,128]{3,2,1,0:T(2,128)(2,1)}, u32[]{:S(2)}) copy-start(bf16[8,16,1,128]{3,2,1,0:T(2,128)(2,1)} %copy-done.56) | copy-start | bytes 98308
  308.7 50.7 %copy-start.59 = (bf16[8,16,1,128]{3,2,1,0:T(2,128)(2,1)S(1)}, bf16[8,16,1,128]{3,2,1,0:T(2,128)(2,1)}, u32[]{:S(2)}) copy-start(bf16[8,16,1,128]{3,2,1,0:T(2,128)(2,1)} %copy-done.58) | copy-start | bytes 98308
  353.9 4.4 collective-permute-start.3
  355.2 3.9 collective-permute-start.2
  373.4 40.8 %all-to-all-start.4 = ((f32[16,1,16,2176]{3,2,1,0:T(8,128)}), f32[16,1,16,2176]{3,2,1,0:T(8,128)S(1)}, u32[]{:S(2)}, u32[]{:S(2)}) async-start(f32[16,1,16,2176]{3,2,1,0:T(8,128)} %broadcast_in_dim.92), calls=%async_computation.4 | async-start | bytes 4456448 | tf_op jit(solution)/shard_map/all_to_all | solution.py:19
  440.7 39.9 %all-to-all-start.5 = ((f32[16,1,16,2176]{3,2,1,0:T(8,128)}), f32[16,1,16,2176]{3,2,1,0:T(8,128)S(1)}, u32[]{:S(2)}, u32[]{:S(2)}) async-start(f32[16,1,16,2176]{3,2,1,0:T(8,128)} %broadcast_in_dim.94), calls=%async_computation.5 | async-start | bytes 4456448 | tf_op jit(solution)/shard_map/all_to_all | solution.py:19
  (58 other events, 1020.4 us)
where the time goes:
time: 493 us; the launch traced here: 484 us
  waiting for transfers between devices  198 us (40%)
  other arithmetic  136 us (28%)
  local copies, waits for them, and re-layouts  67.8 us (14%)
  starting transfers between devices  43.9 us (9%)
  matrix products  30.1 us (6%)
  loops' own time  7.28 us (1%)
    all_to_all x6, waiting for transfers between devices, sent_to_all(): return lax.all_to_all(copies, axis, split_axis=0, concat_axis=0, tiled=True)  197 us
    all_to_all x6, starting transfers between devices, sent_to_all(): return lax.all_to_all(copies, axis, split_axis=0, concat_axis=0, tiled=True)  35 us
    select_n x96, other arithmetic, absorb(): return jnp.where(include, moved, gathered_in)  34.4 us
    dot_general x96, other arithmetic, map_times(): jnp.einsum('cks,ks->cs', chain_map, vectors, precision=lax.Precision.HIGH...  31.9 us
    dynamic_update_slice x48, other arithmetic, run_chain(): _, result = lax.scan(run_advance, inflow, (factor, source), reverse=reverse)  30.4 us
    add x48, other arithmetic, run_advance(): current = source_cell + multiply_cells(factor_cell, current)  30.4 us
    dot_general x48, matrix products, local_advance(): jnp.einsum('cks,kms->cms', factor_cell.astype(jnp.float32), chain_map, pr...  30.1 us
    squeeze x144, local copies, waits for them, and re-layouts, local_map(): lax.scan(local_advance, start, (factor, source), reverse=reverse)  22.4 us
  transfers between devices with their start and end apart: 10, of which 8 were waited for; matrix products, arithmetic and copies ran while one was open for 1% of the time, Pallas kernels for 0%

commit v1 on v0

v1 whole, which is shorter than its diff:
```python
import jax
import jax.numpy as jnp
from jax import lax
from jax.experimental import pallas as pl
from jax.experimental.pallas import tpu as pltpu
from jax.sharding import PartitionSpec as P

SWEEPS = 3
EQ = 16
CELLS = 8
LANES = 128
WALL = 16
SIDE = 4
BLOCK = EQ * EQ
MESH = pl.DeviceIdType.MESH
F32 = jnp.float32

OFFSETS = sorted(
    [(dy, dx) for dy in range(SIDE) for dx in range(SIDE) if dy or dx],
    key=lambda o: -(min(o[0], SIDE - o[0]) + min(o[1], SIDE - o[1])),
)


def rows(start, size):
    return pl.ds(start, size)


def tree_sum(parts):
    while len(parts) > 1:
        parts = [
            parts[k] + parts[k + 1] if k + 1 < len(parts) else parts[k]
            for k in range(0, len(parts), 2)
        ]
    return parts[0]


def times(blocks, base, vectors, at):
    return tree_sum(
        [
            blocks[rows(base + EQ * k, EQ), :] * vectors[rows(at + k, 1), :]
            for k in range(EQ)
        ]
    )


def block_product(out, out_base, left, left_base, right, right_base, add=None, add_base=0):
    def some_columns(step, carry):
        first = pl.multiple_of(step * (4 * EQ), 4 * EQ)
        sums = [None] * 4
        if add is not None:
            sums = [add[rows(add_base + first + EQ * m, EQ), :] for m in range(4)]
        for k in range(EQ):
            column = left[rows(left_base + EQ * k, EQ), :]
            for m in range(4):
                term = column * right[rows(right_base + first + EQ * m + k, 1), :]
                sums[m] = term if sums[m] is None else sums[m] + term
        for m in range(4):
            out[rows(out_base + first + EQ * m, EQ), :] = sums[m]
        return carry

    lax.fori_loop(0, 4, some_columns, 0)


def swap_blocks(values, lane):
    count = len(values)
    width = LANES // count
    half = count // 2
    while half >= 1:
        distance = half * width
        upper = (lane & distance) != 0
        moved = list(values)
        for v in range(count):
            if v & half == 0:
                low, high = values[v], values[v + half]
                moved[v] = jnp.where(upper, pltpu.roll(high, distance, 1), low)
                moved[v + half] = jnp.where(upper, high, pltpu.roll(low, LANES - distance, 1))
        values = moved
        half //= 2
    return values


def kernel(
    rhs, pivot_in, lower_in, upper_in, west_in, east_in, mask_in, codes, out,
    temp, mask_cols, pivot, lower, upper, west, east,
    c_maps, d_maps, b_maps, p_pack, d_pack, b_pack,
    f_rows, q_rows, r_rows, u_rows, uw_rows, ue_rows, s_rows, ab_rows, solve_rows,
    map_out, map_in, vec_out, vec_in, halo_out, halo_in,
    map_send, map_recv, vec_send, vec_recv, halo_send, halo_recv,
):
    me = lax.axis_index("wall")
    stream = lax.axis_index("stream")
    streams = lax.axis_size("stream")
    my_y, my_x = me // SIDE, me % SIDE
    peers = [((my_y + dy) % SIDE) * SIDE + (my_x + dx) % SIDE for dy, dx in OFFSETS]
    next_stream = lax.rem(stream + 1, streams)
    last_stream = lax.rem(stream + streams - 1, streams)
    lane = lax.broadcasted_iota(jnp.int32, (8, LANES), 1)
    lane16 = lax.broadcasted_iota(jnp.int32, (EQ, LANES), 1)

    barrier = pltpu.get_barrier_semaphore()
    for peer in peers:
        pl.semaphore_signal(barrier, inc=1, device_id={"wall": peer}, device_id_type=MESH)
    for other in (next_stream, last_stream):
        pl.semaphore_signal(barrier, inc=1, device_id={"stream": other}, device_id_type=MESH)

    def by_columns(source, target, scale=None):
        def one_cell(j, carry):
            base = pl.multiple_of(j * BLOCK, BLOCK)
            for c in range(EQ):
                temp[rows(base + EQ * c, EQ), :] = source[j, c].astype(F32)
            factor = None if scale is None else scale(j)
            for k in range(EQ):
                column = temp[pl.ds(base + k, EQ, stride=EQ), :]
                if factor is not None:
                    column = column * (mask_cols[EQ * k : EQ * k + EQ, :] * factor)
                target[rows(base + EQ * k, EQ), :] = column
            return carry

        lax.fori_loop(0, CELLS, one_cell, 0)

    by_columns(pivot_in, pivot)
    by_columns(lower_in, lower)
    by_columns(upper_in, upper)

    def forward_cell(j, carry):
        base = pl.multiple_of(j * BLOCK, BLOCK)
        at = pl.multiple_of(j * EQ, EQ)
        f_rows[rows(at, EQ), :] = times(pivot, base, s_rows, at)
        return carry

    def local_chains():
        q_rows[0:EQ, :] = f_rows[0:EQ, :]

        def up(j, carry):
            base = pl.multiple_of(j * BLOCK, BLOCK)
            at = pl.multiple_of(j * EQ, EQ)
            q_rows[rows(at, EQ), :] = f_rows[rows(at, EQ), :] + times(lower, base, q_rows, at - EQ)
            return carry

        lax.fori_loop(1, CELLS, up, 0)
        last = (CELLS - 1) * EQ
        r_rows[last : last + EQ, :] = q_rows[last : last + EQ, :]

        def down(step, carry):
            j = CELLS - 1 - step
            base = pl.multiple_of(j * BLOCK, BLOCK)
            at = pl.multiple_of(j * EQ, EQ)
            r_rows[rows(at, EQ), :] = q_rows[rows(at, EQ), :] + times(upper, base, r_rows, at + EQ)
            return carry

        lax.fori_loop(1, CELLS, down, 0)

    def vec_copy(turn, peer):
        return pltpu.make_async_remote_copy(
            src_ref=vec_out.at[turn, peer // SIDE],
            dst_ref=vec_in.at[turn, me],
            send_sem=vec_send.at[turn, peer],
            recv_sem=vec_recv.at[turn, me],
            device_id={"wall": peer},
            device_id_type=MESH,
        )

    def vec_arrival(turn, peer):
        return pltpu.make_async_remote_copy(
            src_ref=vec_out.at[turn, 0],
            dst_ref=vec_in.at[turn, peer],
            send_sem=vec_send.at[turn, peer],
            recv_sem=vec_recv.at[turn, peer],
            device_id={"wall": peer},
            device_id_type=MESH,
        )

    def send_vectors(turn, values):
        for u, value in enumerate(swap_blocks(values, lane)):
            vec_out[turn, u] = value
        for peer in peers:
            vec_copy(turn, peer).start()
        vec_in[turn, me] = vec_out[turn, my_y]

    def take_vectors(turn):
        for peer in peers:
            vec_arrival(turn, peer).wait_recv()
        for peer in peers:
            vec_copy(turn, peer).wait_send()
        gathered = []
        slot = (lane // 8) % SIDE
        for high in range(SIDE):
            chosen = None
            for low in range(SIDE):
                shift = (8 * (low - my_x) + LANES) % LANES
                piece = pltpu.roll(vec_in[turn, SIDE * high + low], shift, 1)
                chosen = piece if chosen is None else jnp.where(slot == low, piece, chosen)
            gathered.append(chosen)
        return swap_blocks(gathered, lane)

    def map_copy(which, peer):
        return pltpu.make_async_remote_copy(
            src_ref=map_out.at[which, peer],
            dst_ref=map_in.at[which, me],
            send_sem=map_send.at[which, peer],
            recv_sem=map_recv.at[which, me],
            device_id={"wall": peer},
            device_id_type=MESH,
        )

    def map_arrival(which, peer):
        return pltpu.make_async_remote_copy(
            src_ref=map_out.at[which, peer],
            dst_ref=map_in.at[which, peer],
            send_sem=map_send.at[which, peer],
            recv_sem=map_recv.at[which, peer],
            device_id={"wall": peer},
            device_id_type=MESH,
        )

    def send_map(which, maps, base):
        def one_half(half, carry):
            at = pl.multiple_of(half * 8, 8)
            values = [maps[rows(base + EQ * m + at, 8), :] for m in range(EQ)]
            for g, value in enumerate(swap_blocks(values, lane)):
                map_out[which, g, rows(at, 8), :] = value
            return carry

        lax.fori_loop(0, 2, one_half, 0)
        for peer in peers:
            map_copy(which, peer).start()
        map_in[which, me] = map_out[which, me]

    def take_map(which, packed, keep):
        for peer in peers:
            map_arrival(which, peer).wait_recv()
        for peer in peers:
            map_copy(which, peer).wait_send()

        def one_half(half, carry):
            at = pl.multiple_of(half * 8, 8)
            values = [map_in[which, i, rows(at, 8), :] for i in range(WALL)]
            for m, value in enumerate(swap_blocks(values, lane)):
                if keep is not None:
                    value = jnp.where(keep, value, 0.0)
                packed[rows(EQ * m + at, 8), :] = value
            return carry

        lax.fori_loop(0, 2, one_half, 0)

    for j in range(CELLS):
        s_rows[EQ * j : EQ * j + EQ, :] = rhs[j]
    lax.fori_loop(0, CELLS, forward_cell, 0)
    local_chains()
    top = (CELLS - 1) * EQ

    def edge_vectors():
        return [
            q_rows[top : top + 8, :],
            q_rows[top + 8 : top + 16, :],
            r_rows[0:8, :],
            r_rows[8:16, :],
        ]

    pl.semaphore_wait(barrier, len(peers) + 2)
    send_vectors(0, edge_vectors())

    c_maps[0:BLOCK, :] = lower[0:BLOCK, :]
    d_maps[(CELLS - 1) * BLOCK : CELLS * BLOCK, :] = upper[(CELLS - 1) * BLOCK : CELLS * BLOCK, :]

    def c_cell(j, carry):
        base = pl.multiple_of(j * BLOCK, BLOCK)
        block_product(c_maps, base, lower, base, c_maps, base - BLOCK)
        return carry

    lax.fori_loop(1, CELLS, c_cell, 0)
    send_map(0, c_maps, (CELLS - 1) * BLOCK)

    def d_cell(step, carry):
        base = pl.multiple_of((CELLS - 1 - step) * BLOCK, BLOCK)
        block_product(d_maps, base, upper, base, d_maps, base + BLOCK)
        return carry

    lax.fori_loop(1, CELLS, d_cell, 0)
    send_map(1, d_maps, 0)
    final = (CELLS - 1) * BLOCK
    b_maps[final : final + BLOCK, :] = c_maps[final : final + BLOCK, :]

    def b_cell(step, carry):
        base = pl.multiple_of((CELLS - 1 - step) * BLOCK, BLOCK)
        block_product(b_maps, base, upper, base, b_maps, base + BLOCK, c_maps, base)
        return carry

    lax.fori_loop(1, CELLS, b_cell, 0)
    send_map(2, b_maps, 0)

    for k in range(EQ):
        column = mask_in[:, k : k + 1].astype(F32)
        mask_cols[EQ * k : EQ * k + EQ, :] = jnp.broadcast_to(column, (EQ, LANES))

    def west_on(j):
        code = codes[rows(j, 1), :]
        return jnp.where((code == 0) | (code == 1), 1.0, 0.0).astype(F32)

    def east_on(j):
        code = codes[rows(j, 1), :]
        return jnp.where((code == 0) | (code == 2), 1.0, 0.0).astype(F32)

    by_columns(west_in, west, west_on)
    by_columns(east_in, east, east_on)

    first_group = lane < 8
    take_map(0, p_pack, jnp.logical_not(first_group))
    take_map(1, d_pack, lane < LANES - 8)
    take_map(2, b_pack, jnp.logical_not(first_group))

    def halo_copy(sweep, side, other):
        return pltpu.make_async_remote_copy(
            src_ref=halo_out.at[sweep, side],
            dst_ref=halo_in.at[sweep, side],
            send_sem=halo_send.at[sweep, side],
            recv_sem=halo_recv.at[sweep, side],
            device_id={"stream": other},
            device_id_type=MESH,
        )

    def one_sweep(sweep, carry):
        q_low, q_high, r_low, r_high = take_vectors(0)

        solve_rows[0:8, :] = pltpu.roll(q_low, 8, 1)
        solve_rows[8:16, :] = pltpu.roll(q_high, 8, 1)
        q_all = jnp.concatenate([q_low, q_high], axis=0)
        r_all = jnp.concatenate([r_low, r_high], axis=0)

        def rise(step, carry):
            outflow = q_all + times(p_pack, 0, solve_rows, 0)
            solve_rows[0:EQ, :] = pltpu.roll(outflow, 8, 1)
            return carry

        lax.fori_loop(0, WALL - 2, rise, 0)
        down_all = r_all + times(b_pack, 0, solve_rows, 0)
        solve_rows[EQ : 2 * EQ, :] = pltpu.roll(down_all, LANES - 8, 1)

        def fall(step, carry):
            outflow = down_all + times(d_pack, 0, solve_rows, EQ)
            solve_rows[EQ : 2 * EQ, :] = pltpu.roll(outflow, LANES - 8, 1)
            return carry

        lax.fori_loop(0, WALL - 2, fall, 0)
        a_all = jnp.where(lane16 < 8, 0.0, solve_rows[0:EQ, :])
        b_all = jnp.where(lane16 < LANES - 8, solve_rows[EQ : 2 * EQ, :], 0.0)
        send_vectors(1, [a_all[0:8], a_all[8:16], b_all[0:8], b_all[8:16]])
        for v, value in enumerate(take_vectors(1)):
            ab_rows[8 * v : 8 * v + 8, :] = value

        def update_cell(j, carry):
            base = pl.multiple_of(j * BLOCK, BLOCK)
            at = pl.multiple_of(j * EQ, EQ)
            u_rows[rows(at, EQ), :] = (
                r_rows[rows(at, EQ), :]
                + times(b_maps, base, ab_rows, 0)
                + times(d_maps, base, ab_rows, EQ)
            )
            return carry

        lax.fori_loop(0, CELLS, update_cell, 0)

        @pl.when(sweep < SWEEPS - 1)
        def _():
            to_east = jnp.zeros((EQ, LANES), F32)
            to_west = jnp.zeros((EQ, LANES), F32)
            for j in range(CELLS):
                value = u_rows[EQ * j : EQ * j + EQ, :]
                to_east = jnp.where(lane16 == j, pltpu.roll(value, j + 1, 1), to_east)
                to_west = jnp.where(lane16 == j, pltpu.roll(value, j, 1) if j else value, to_west)
            halo_out[sweep, 0] = to_east
            halo_out[sweep, 1] = to_west
            halo_copy(sweep, 0, next_stream).start()
            halo_copy(sweep, 1, last_stream).start()
            halo_copy(sweep, 0, next_stream).wait()
            halo_copy(sweep, 1, last_stream).wait()
            from_west = jnp.where(stream == 0, 0.0, halo_in[sweep, 0])
            from_east = jnp.where(stream == streams - 1, 0.0, halo_in[sweep, 1])
            for j in range(CELLS):
                value = u_rows[EQ * j : EQ * j + EQ, :]
                ghost = pltpu.roll(from_west, LANES - j, 1) if j else from_west
                uw_rows[EQ * j : EQ * j + EQ, :] = jnp.where(
                    lane16 == 0, ghost, pltpu.roll(value, 1, 1)
                )
                ghost = pltpu.roll(from_east, LANES - 1 - j, 1)
                ue_rows[EQ * j : EQ * j + EQ, :] = jnp.where(
                    lane16 == LANES - 1, ghost, pltpu.roll(value, LANES - 1, 1)
                )

            def source_cell(j, carry):
                base = pl.multiple_of(j * BLOCK, BLOCK)
                at = pl.multiple_of(j * EQ, EQ)
                s_rows[rows(at, EQ), :] = (
                    rhs[j] - times(west, base, uw_rows, at) - times(east, base, ue_rows, at)
                )
                return carry

            lax.fori_loop(0, CELLS, source_cell, 0)
            lax.fori_loop(0, CELLS, forward_cell, 0)
            local_chains()
            send_vectors(0, edge_vectors())

        return carry

    lax.fori_loop(0, SWEEPS, one_sweep, 0)
    for j in range(CELLS):
        out[j] = u_rows[EQ * j : EQ * j + EQ, :]


def on_device(*arrays):
    big = pltpu.VMEM((CELLS * BLOCK, LANES), F32)
    block = pltpu.VMEM((BLOCK, LANES), F32)
    vectors = pltpu.VMEM((CELLS * EQ, LANES), F32)
    pair = pltpu.VMEM((2 * EQ, LANES), F32)
    return pl.pallas_call(
        kernel,
        out_shape=jax.ShapeDtypeStruct((CELLS, EQ, LANES), F32),
        in_specs=[pl.BlockSpec(memory_space=pltpu.VMEM)] * 8,
        out_specs=pl.BlockSpec(memory_space=pltpu.VMEM),
        scratch_shapes=[
            big, block, big, big, big, big, big,
            big, big, big, block, block, block,
            vectors, vectors, vectors, vectors, vectors, vectors, vectors, pair, pair,
            pltpu.VMEM((3, WALL, EQ, LANES), F32),
            pltpu.VMEM((3, WALL, EQ, LANES), F32),
            pltpu.VMEM((2, SIDE, 8, LANES), F32),
            pltpu.VMEM((2, WALL, 8, LANES), F32),
            pltpu.VMEM((SWEEPS - 1, 2, EQ, LANES), F32),
            pltpu.VMEM((SWEEPS - 1, 2, EQ, LANES), F32),
            pltpu.SemaphoreType.DMA((3, WALL)),
            pltpu.SemaphoreType.DMA((3, WALL)),
            pltpu.SemaphoreType.DMA((2, WALL)),
            pltpu.SemaphoreType.DMA((2, WALL)),
            pltpu.SemaphoreType.DMA((SWEEPS - 1, 2)),
            pltpu.SemaphoreType.DMA((SWEEPS - 1, 2)),
        ],
        compiler_params=pltpu.CompilerParams(collective_id=0, has_side_effects=True),
    )(*arrays)


def solution(mesh):
    return jax.shard_map(
        on_device,
        mesh=mesh,
        in_specs=(
            P("wall", None, "stream"),
            P("wall", None, None, "stream"),
            P("wall", None, None, "stream"),
            P("wall", None, None, "stream"),
            P("wall", None, None, "stream"),
            P("wall", None, None, "stream"),
            P(),
            P("wall", "stream"),
        ),
        out_specs=P("wall", None, "stream"),
        check_vma=False,
    )
```

time: 493 us -> 63.1 us (0.13); the launches traced: 484 us -> 63 us
  waiting for transfers between devices: 198 us -> 0 us
  other arithmetic: 136 us -> 0 us
  local copies, waits for them, and re-layouts: 67.8 us -> 1.47 us
  Pallas kernels: 0 us -> 61.5 us
  starting transfers between devices: 43.9 us -> 0 us
  matrix products: 30.1 us -> 0 us
  loops' own time: 7.28 us -> 0 us
    all_to_all x6 -> x0, waiting for transfers between devices: 197 us -> none  [sent_to_all(): return lax.all_to_all(copies, axis, split_axis=0, concat_axis=0, tiled=True)]
    pallas_call x0 -> x1, Pallas kernels: none -> 61.5 us  [on_device(): pl.pallas_call(kernel, out_shape=jax.ShapeDtypeStruct((CELLS, EQ, LANES),...]
    all_to_all x6 -> x0, starting transfers between devices: 35 us -> none  [sent_to_all(): return lax.all_to_all(copies, axis, split_axis=0, concat_axis=0, tiled=True)]
    select_n x96 -> x0, other arithmetic: 34.4 us -> none  [absorb(): return jnp.where(include, moved, gathered_in)]
    add x99 -> x0, other arithmetic: 32.6 us -> none  [the longest x48 30.4 us: run_advance(): current = source_cell + multiply_cells(factor_cell, current)]
    dot_general x96 -> x0, other arithmetic: 31.9 us -> none  [map_times(): jnp.einsum('cks,ks->cs', chain_map, vectors, precision=lax.Precision.HIGH...]
    dynamic_update_slice x48 -> x0, other arithmetic: 30.4 us -> none  [run_chain(): _, result = lax.scan(run_advance, inflow, (factor, source), reverse=reverse)]
    dot_general x48 -> x0, matrix products: 30.1 us -> none  [local_advance(): jnp.einsum('cks,kms->cms', factor_cell.astype(jnp.float32), chain_map, pr...]
  transfers between devices with their start and end apart: 10 -> 0, of which waited for: 8 -> 0; matrix products, arithmetic and copies ran while one was open for 1% -> 0% of each run, Pallas kernels for 0% -> 0%
where the time goes in v1:
time: 63.1 us; the launch traced here: 63 us
  Pallas kernels  61.5 us (97%)
  local copies, waits for them, and re-layouts  1.47 us (2%)
    pallas_call x1, Pallas kernels, on_device(): pl.pallas_call(kernel, out_shape=jax.ShapeDtypeStruct((CELLS, EQ, LANES),...  61.5 us
    unnamed x1, local copies, waits for them, and re-layouts  1.47 us

profile of v1, /device:TPU:8, one launch (start us, length us, event | category | flops | bytes accessed | tf_op | source)
XLA Modules:
  0.0 63.0 jit_solution(14141260764972361582)
XLA Ops:
  0.0 61.5 %shard_map.82 = f32[8,16,128]{2,1,0:T(8,128)} custom-call(f32[8,16,128]{2,1,0:T(8,128)} %rhs.1, bf16[8,16,16,128]{3,2,1,0:T(8,128)(2,1)} %pivot_in.1, bf16[8,16,16,128]{3,2,1,0:T(8,128)(2,1)} %lower_in.1, bf16[8,16,16,128]{3,2,1,0:T(8,128)(2,1)} %upper_in.1, bf16[8,16,16,128]{3,2,1,0:T(8,128)(2,1)} %west_in.1, bf16[8,16,16,128]{3,2,1,0:T(8,128)(2,1)} %east_in.1, ...), custom_call_target="tpu_custom_call" | custom-call | tf_op jit(solution)/shard_map/pallas_call | solution.py:415
  61.5 1.5 %copy.10 = f32[8,16,128]{2,1,0:T(8,128)} copy(f32[8,16,128]{2,1,0:T(8,128)} %shard_map.82) | data formatting | bytes 131072

commit v2 on v1

v2 whole, which is shorter than its diff:
```python
import jax
import jax.numpy as jnp
from jax import lax
from jax.experimental import pallas as pl
from jax.experimental.pallas import tpu as pltpu
from jax.sharding import PartitionSpec as P

SWEEPS = 3
EQ = 16
CELLS = 8
LANES = 128
WALL = 16
SIDE = 4
BLOCK = EQ * EQ
MESH = pl.DeviceIdType.MESH
F32 = jnp.float32

OFFSETS = sorted(
    [(dy, dx) for dy in range(SIDE) for dx in range(SIDE) if dy or dx],
    key=lambda o: -(min(o[0], SIDE - o[0]) + min(o[1], SIDE - o[1])),
)


def rows(start, size):
    return pl.ds(start, size)


def tree_sum(parts):
    while len(parts) > 1:
        parts = [
            parts[k] + parts[k + 1] if k + 1 < len(parts) else parts[k]
            for k in range(0, len(parts), 2)
        ]
    return parts[0]


def times(blocks, base, vectors, at):
    return tree_sum(
        [
            blocks[rows(base + EQ * k, EQ), :] * vectors[rows(at + k, 1), :]
            for k in range(EQ)
        ]
    )


def block_product(out, out_base, left, left_base, right, right_base, add=None, add_base=0):
    def some_columns(step, carry):
        first = pl.multiple_of(step * (4 * EQ), 4 * EQ)
        sums = [None] * 4
        if add is not None:
            sums = [add[rows(add_base + first + EQ * m, EQ), :] for m in range(4)]
        for k in range(EQ):
            column = left[rows(left_base + EQ * k, EQ), :]
            for m in range(4):
                term = column * right[rows(right_base + first + EQ * m + k, 1), :]
                sums[m] = term if sums[m] is None else sums[m] + term
        for m in range(4):
            out[rows(out_base + first + EQ * m, EQ), :] = sums[m]
        return carry

    lax.fori_loop(0, 4, some_columns, 0)


def swap_four(values, slot, width):
    moved = []
    for u in range(SIDE):
        total = None
        for v in range(SIDE):
            piece = values[v] if u == v else pltpu.roll(values[v], (width * (v - u)) % LANES, 1)
            total = piece if total is None else jnp.where(slot == v, piece, total)
        moved.append(total)
    return moved


def kernel(
    rhs_hbm, pivot_hbm, lower_hbm, upper_hbm, west_hbm, east_hbm, mask_in, codes, out,
    rhs, pivot_in, lower_in, upper_in, west_in, east_in,
    temp, mask_cols, pivot, lower, upper, west, east, c_maps, d_maps, b_maps, others,
    f_rows, q_rows, r_rows, uw_rows, ue_rows, s_rows, ab_rows,
    q_all, r_all, a_all, b_all,
    map_out, map_in, up_out, up_in, back_out, back_in, halo_out, halo_in,
    load_sem, map_send, map_recv, vec_send, vec_recv, halo_send, halo_recv,
):
    me = lax.axis_index("wall")
    stream = lax.axis_index("stream")
    streams = lax.axis_size("stream")
    my_y, my_x = me // SIDE, me % SIDE
    peers = [((my_y + dy) % SIDE) * SIDE + (my_x + dx) % SIDE for dy, dx in OFFSETS]
    next_stream = lax.rem(stream + 1, streams)
    last_stream = lax.rem(stream + streams - 1, streams)
    lane = lax.broadcasted_iota(jnp.int32, (8, LANES), 1)
    lane16 = lax.broadcasted_iota(jnp.int32, (EQ, LANES), 1)
    high_slot, low_slot = lane // 32, (lane // 8) % SIDE

    loads = [
        pltpu.make_async_copy(source, target, load_sem.at[k])
        for k, (source, target) in enumerate(
            [
                (lower_hbm, lower_in),
                (upper_hbm, upper_in),
                (pivot_hbm, pivot_in),
                (rhs_hbm, rhs),
                (west_hbm, west_in),
                (east_hbm, east_in),
            ]
        )
    ]
    for load in loads:
        load.start()

    barrier = pltpu.get_barrier_semaphore()
    for peer in peers:
        pl.semaphore_signal(barrier, inc=1, device_id={"wall": peer}, device_id_type=MESH)
    for other in (next_stream, last_stream):
        pl.semaphore_signal(barrier, inc=1, device_id={"stream": other}, device_id_type=MESH)

    def by_columns(load, source, target, scale=None):
        load.wait()

        def one_cell(j, carry):
            base = pl.multiple_of(j * BLOCK, BLOCK)
            for c in range(EQ):
                temp[rows(base + EQ * c, EQ), :] = source[j, c].astype(F32)
            factor = None if scale is None else scale(j)
            for k in range(EQ):
                column = temp[pl.ds(base + k, EQ, stride=EQ), :]
                if factor is not None:
                    column = column * (mask_cols[EQ * k : EQ * k + EQ, :] * factor)
                target[rows(base + EQ * k, EQ), :] = column
            return carry

        lax.fori_loop(0, CELLS, one_cell, 0)

    def map_copy(which, peer):
        return pltpu.make_async_remote_copy(
            src_ref=map_out.at[which, peer],
            dst_ref=map_in.at[which, me],
            send_sem=map_send.at[which, peer],
            recv_sem=map_recv.at[which, me],
            device_id={"wall": peer},
            device_id_type=MESH,
        )

    def map_arrival(which, peer):
        return pltpu.make_async_remote_copy(
            src_ref=map_out.at[which, peer],
            dst_ref=map_in.at[which, peer],
            send_sem=map_send.at[which, peer],
            recv_sem=map_recv.at[which, peer],
            device_id={"wall": peer},
            device_id_type=MESH,
        )

    def send_map(which, maps, base):
        for half in range(2):
            grid = [
                [maps[rows(base + EQ * (SIDE * high + low) + 8 * half, 8), :] for high in range(SIDE)]
                for low in range(SIDE)
            ]
            grid = [swap_four(values, high_slot, 32) for values in grid]
            for high in range(SIDE):
                values = swap_four([grid[low][high] for low in range(SIDE)], low_slot, 8)
                for low, value in enumerate(values):
                    map_out[which, SIDE * high + low, 8 * half : 8 * half + 8, :] = value
        for peer in peers:
            map_copy(which, peer).start()
        map_in[which, me] = map_out[which, me]

    def take_map(which, carry):
        for peer in peers:
            map_arrival(which, peer).wait_recv()
        for peer in peers:
            map_copy(which, peer).wait_send()
        shifts = [(8 * (my_x - m) + LANES) % LANES for m in range(EQ)]
        for i in range(WALL):
            value = map_in[which, i]
            for m in range(EQ):
                at = pl.multiple_of(which * (WALL * BLOCK) + BLOCK * i + EQ * m, EQ)
                others[rows(at, EQ), :] = pltpu.roll(value, shifts[m], 1)
        return carry

    by_columns(loads[0], lower_in, lower)
    c_maps[0:BLOCK, :] = lower[0:BLOCK, :]

    def c_cell(j, carry):
        base = pl.multiple_of(j * BLOCK, BLOCK)
        block_product(c_maps, base, lower, base, c_maps, base - BLOCK)
        return carry

    lax.fori_loop(1, CELLS, c_cell, 0)
    pl.semaphore_wait(barrier, len(peers) + 2)
    send_map(0, c_maps, (CELLS - 1) * BLOCK)

    by_columns(loads[1], upper_in, upper)
    d_maps[(CELLS - 1) * BLOCK : CELLS * BLOCK, :] = upper[(CELLS - 1) * BLOCK : CELLS * BLOCK, :]
    final = (CELLS - 1) * BLOCK
    b_maps[final : final + BLOCK, :] = c_maps[final : final + BLOCK, :]

    def b_cell(step, carry):
        base = pl.multiple_of((CELLS - 1 - step) * BLOCK, BLOCK)
        block_product(b_maps, base, upper, base, b_maps, base + BLOCK, c_maps, base)
        return carry

    lax.fori_loop(1, CELLS, b_cell, 0)
    send_map(1, b_maps, 0)

    def d_cell(step, carry):
        base = pl.multiple_of((CELLS - 1 - step) * BLOCK, BLOCK)
        block_product(d_maps, base, upper, base, d_maps, base + BLOCK)
        return carry

    lax.fori_loop(1, CELLS, d_cell, 0)
    send_map(2, d_maps, 0)

    def forward_cell(j):
        block = jnp.minimum(j, CELLS - 1)
        base = pl.multiple_of(block * BLOCK, BLOCK)
        at = pl.multiple_of(j * EQ, EQ)
        f_rows[rows(at, EQ), :] = times(pivot, base, s_rows, at)

    def up_cell(j):
        base = pl.multiple_of(j * BLOCK, BLOCK)
        at = pl.multiple_of(j * EQ, EQ)
        q_rows[rows(at, EQ), :] = f_rows[rows(at, EQ), :] + times(lower, base, q_rows, at - EQ)

    def down_chain():
        last = (CELLS - 1) * EQ
        r_rows[last : last + EQ, :] = q_rows[last : last + EQ, :]

        def down(step, carry):
            j = CELLS - 1 - step
            base = pl.multiple_of(j * BLOCK, BLOCK)
            at = pl.multiple_of(j * EQ, EQ)
            r_rows[rows(at, EQ), :] = q_rows[rows(at, EQ), :] + times(upper, base, r_rows, at + EQ)
            return carry

        lax.fori_loop(1, CELLS, down, 0)

    def up_copy(peer):
        return pltpu.make_async_remote_copy(
            src_ref=up_out.at[peer // SIDE],
            dst_ref=up_in.at[me],
            send_sem=vec_send.at[0, peer],
            recv_sem=vec_recv.at[0, me],
            device_id={"wall": peer},
            device_id_type=MESH,
        )

    def up_arrival(peer):
        return pltpu.make_async_remote_copy(
            src_ref=up_out.at[0],
            dst_ref=up_in.at[peer],
            send_sem=vec_send.at[0, peer],
            recv_sem=vec_recv.at[0, peer],
            device_id={"wall": peer},
            device_id_type=MESH,
        )

    def back_copy(peer):
        return pltpu.make_async_remote_copy(
            src_ref=back_out.at[peer],
            dst_ref=back_in.at[me],
            send_sem=vec_send.at[1, peer],
            recv_sem=vec_recv.at[1, me],
            device_id={"wall": peer},
            device_id_type=MESH,
        )

    def back_arrival(peer):
        return pltpu.make_async_remote_copy(
            src_ref=back_out.at[peer],
            dst_ref=back_in.at[peer],
            send_sem=vec_send.at[1, peer],
            recv_sem=vec_recv.at[1, peer],
            device_id={"wall": peer},
            device_id_type=MESH,
        )

    def send_up():
        top = (CELLS - 1) * EQ
        values = [
            q_rows[top : top + 8, :],
            q_rows[top + 8 : top + 16, :],
            r_rows[0:8, :],
            r_rows[8:16, :],
        ]
        for u, value in enumerate(swap_four(values, high_slot, 32)):
            up_out[u] = value
        for peer in peers:
            up_copy(peer).start()
        up_in[me] = up_out[my_y]

    def take_up():
        for peer in peers:
            up_arrival(peer).wait_recv()
        for peer in peers:
            up_copy(peer).wait_send()
        for i in range(WALL):
            tile = up_in[i]
            q_all[EQ * i : EQ * i + 8, :] = tile
            q_all[EQ * i + 8 : EQ * i + 16, :] = pltpu.roll(tile, LANES - 32, 1)
            r_all[EQ * i : EQ * i + 8, :] = pltpu.roll(tile, LANES - 64, 1)
            r_all[EQ * i + 8 : EQ * i + 16, :] = pltpu.roll(tile, LANES - 96, 1)

    def send_back():
        for i in range(WALL):
            tile = a_all[EQ * i : EQ * i + 8, :]
            for v, piece in enumerate(
                [
                    a_all[EQ * i + 8 : EQ * i + 16, :],
                    b_all[EQ * i : EQ * i + 8, :],
                    b_all[EQ * i + 8 : EQ * i + 16, :],
                ]
            ):
                tile = jnp.where(high_slot == v + 1, pltpu.roll(piece, 32 * (v + 1), 1), tile)
            back_out[i] = tile
        for peer in peers:
            back_copy(peer).start()
        back_in[me] = back_out[me]

    def take_back():
        for peer in peers:
            back_arrival(peer).wait_recv()
        for peer in peers:
            back_copy(peer).wait_send()
        values = []
        for high in range(SIDE):
            total = back_in[SIDE * high]
            for low in range(1, SIDE):
                total = jnp.where(low_slot == low, back_in[SIDE * high + low], total)
            values.append(total)
        for v, value in enumerate(swap_four(values, high_slot, 32)):
            ab_rows[8 * v : 8 * v + 8, :] = value

    by_columns(loads[2], pivot_in, pivot)
    loads[3].wait()
    for j in range(CELLS):
        s_rows[EQ * j : EQ * j + EQ, :] = rhs[j]
    forward_cell(0)
    q_rows[0:EQ, :] = f_rows[0:EQ, :]
    forward_cell(1)

    def first_up(j, carry):
        up_cell(j)
        forward_cell(j + 1)
        return carry

    lax.fori_loop(1, CELLS, first_up, 0)
    down_chain()
    send_up()

    for k in range(EQ):
        column = mask_in[:, k : k + 1].astype(F32)
        mask_cols[EQ * k : EQ * k + EQ, :] = jnp.broadcast_to(column, (EQ, LANES))

    def west_on(j):
        code = codes[rows(j, 1), :]
        return jnp.where((code == 0) | (code == 1), 1.0, 0.0).astype(F32)

    def east_on(j):
        code = codes[rows(j, 1), :]
        return jnp.where((code == 0) | (code == 2), 1.0, 0.0).astype(F32)

    by_columns(loads[4], west_in, west, west_on)
    by_columns(loads[5], east_in, east, east_on)
    a_all[0:EQ, :] = jnp.zeros((EQ, LANES), F32)
    b_all[(WALL - 1) * EQ : WALL * EQ, :] = jnp.zeros((EQ, LANES), F32)
    lax.fori_loop(0, 3, take_map, 0)

    def halo_copy(sweep, side, other):
        return pltpu.make_async_remote_copy(
            src_ref=halo_out.at[sweep, side],
            dst_ref=halo_in.at[sweep, side],
            send_sem=halo_send.at[sweep, side],
            recv_sem=halo_recv.at[sweep, side],
            device_id={"stream": other},
            device_id_type=MESH,
        )

    def source_cell(j):
        block = jnp.minimum(j, CELLS - 1)
        base = pl.multiple_of(block * BLOCK, BLOCK)
        at = pl.multiple_of(block * EQ, EQ)
        s_rows[rows(pl.multiple_of(j * EQ, EQ), EQ), :] = (
            rhs[block] - times(west, base, uw_rows, at) - times(east, base, ue_rows, at)
        )

    def one_sweep(sweep, carry):
        take_up()

        a_all[EQ : 2 * EQ, :] = q_all[0:EQ, :]
        maps_b, maps_d = WALL * BLOCK, 2 * WALL * BLOCK

        def rise(i, carry):
            at = pl.multiple_of(i * EQ, EQ)
            base = pl.multiple_of(i * BLOCK, BLOCK)
            a_all[rows(at + EQ, EQ), :] = q_all[rows(at, EQ), :] + times(others, base, a_all, at)
            r_all[rows(at, EQ), :] = r_all[rows(at, EQ), :] + times(others, maps_b + base, a_all, at)
            return carry

        lax.fori_loop(1, WALL - 1, rise, 0)
        last = (WALL - 1) * EQ
        b_all[last - EQ : last, :] = r_all[last : last + EQ, :] + times(
            others, maps_b + (WALL - 1) * BLOCK, a_all, last
        )

        def fall(step, carry):
            i = WALL - 1 - step
            at = pl.multiple_of(i * EQ, EQ)
            base = pl.multiple_of(i * BLOCK, BLOCK)
            b_all[rows(at - EQ, EQ), :] = r_all[rows(at, EQ), :] + times(others, maps_d + base, b_all, at)
            return carry

        lax.fori_loop(1, WALL - 1, fall, 0)
        send_back()
        take_back()

        def update_cell(j, carry):
            base = pl.multiple_of(j * BLOCK, BLOCK)
            at = pl.multiple_of(j * EQ, EQ)
            out[j] = (
                r_rows[rows(at, EQ), :]
                + times(b_maps, base, ab_rows, 0)
                + times(d_maps, base, ab_rows, EQ)
            )
            return carry

        lax.fori_loop(0, CELLS, update_cell, 0)

        @pl.when(sweep < SWEEPS - 1)
        def _():
            to_east = pltpu.roll(out[0], 1, 1)
            to_west = out[0]
            for j in range(1, CELLS):
                to_east = jnp.where(lane16 == j, pltpu.roll(out[j], j + 1, 1), to_east)
                to_west = jnp.where(lane16 == j, pltpu.roll(out[j], j, 1), to_west)
            halo_out[sweep, 0] = to_east
            halo_out[sweep, 1] = to_west
            halo_copy(sweep, 0, next_stream).start()
            halo_copy(sweep, 1, last_stream).start()
            for j in range(CELLS):
                uw_rows[EQ * j : EQ * j + EQ, :] = pltpu.roll(out[j], 1, 1)
                ue_rows[EQ * j : EQ * j + EQ, :] = pltpu.roll(out[j], LANES - 1, 1)
            halo_copy(sweep, 0, next_stream).wait()
            halo_copy(sweep, 1, last_stream).wait()
            from_west = jnp.where(stream == 0, 0.0, halo_in[sweep, 0])
            from_east = jnp.where(stream == streams - 1, 0.0, halo_in[sweep, 1])
            for j in range(CELLS):
                part = slice(EQ * j, EQ * j + EQ)
                ghost = pltpu.roll(from_west, LANES - j, 1) if j else from_west
                uw_rows[part, :] = jnp.where(lane16 == 0, ghost, uw_rows[part, :])
                ghost = pltpu.roll(from_east, LANES - 1 - j, 1)
                ue_rows[part, :] = jnp.where(lane16 == LANES - 1, ghost, ue_rows[part, :])

            source_cell(0)
            source_cell(1)
            forward_cell(0)
            q_rows[0:EQ, :] = f_rows[0:EQ, :]
            source_cell(2)
            forward_cell(1)

            def next_up(j, carry):
                up_cell(j)
                forward_cell(j + 1)
                source_cell(j + 2)
                return carry

            lax.fori_loop(1, CELLS, next_up, 0)
            down_chain()
            send_up()

        return carry

    lax.fori_loop(0, SWEEPS, one_sweep, 0)


def on_device(*arrays):
    big = pltpu.VMEM((CELLS * BLOCK, LANES), F32)
    block = pltpu.VMEM((BLOCK, LANES), F32)
    vectors = pltpu.VMEM((CELLS * EQ, LANES), F32)
    padded = pltpu.VMEM(((CELLS + 2) * EQ, LANES), F32)
    pair = pltpu.VMEM((2 * EQ, LANES), F32)
    wall = pltpu.VMEM((WALL * EQ, LANES), F32)
    narrow = pltpu.VMEM((CELLS, EQ, EQ, LANES), jnp.bfloat16)
    tiles = pltpu.VMEM((WALL, 8, LANES), F32)
    return pl.pallas_call(
        kernel,
        out_shape=jax.ShapeDtypeStruct((CELLS, EQ, LANES), F32),
        in_specs=[pl.BlockSpec(memory_space=pl.ANY)] * 6
        + [pl.BlockSpec(memory_space=pltpu.VMEM)] * 2,
        out_specs=pl.BlockSpec(memory_space=pltpu.VMEM),
        scratch_shapes=[
            pltpu.VMEM((CELLS, EQ, LANES), F32), narrow, narrow, narrow, narrow, narrow,
            big, block, big, big, big, big, big, big, big, big,
            pltpu.VMEM((3 * WALL * BLOCK, LANES), F32),
            padded, vectors, vectors, vectors, vectors, padded, pair,
            wall, wall, wall, wall,
            pltpu.VMEM((3, WALL, EQ, LANES), F32),
            pltpu.VMEM((3, WALL, EQ, LANES), F32),
            pltpu.VMEM((SIDE, 8, LANES), F32), tiles, tiles, tiles,
            pltpu.VMEM((SWEEPS - 1, 2, EQ, LANES), F32),
            pltpu.VMEM((SWEEPS - 1, 2, EQ, LANES), F32),
            pltpu.SemaphoreType.DMA((6,)),
            pltpu.SemaphoreType.DMA((3, WALL)),
            pltpu.SemaphoreType.DMA((3, WALL)),
            pltpu.SemaphoreType.DMA((2, WALL)),
            pltpu.SemaphoreType.DMA((2, WALL)),
            pltpu.SemaphoreType.DMA((SWEEPS - 1, 2)),
            pltpu.SemaphoreType.DMA((SWEEPS - 1, 2)),
        ],
        compiler_params=pltpu.CompilerParams(collective_id=0, has_side_effects=True),
    )(*arrays)


def solution(mesh):
    return jax.shard_map(
        on_device,
        mesh=mesh,
        in_specs=(
            P("wall", None, "stream"),
            P("wall", None, None, "stream"),
            P("wall", None, None, "stream"),
            P("wall", None, None, "stream"),
            P("wall", None, None, "stream"),
            P("wall", None, None, "stream"),
            P(),
            P("wall", "stream"),
        ),
        out_specs=P("wall", None, "stream"),
        check_vma=False,
    )
```

time: 63.1 us -> 53.7 us (0.85)
  Pallas kernels: 61.5 us -> 52 us
    pallas_call x1, Pallas kernels: 61.5 us -> 52 us  [on_device(): pl.pallas_call(kernel, out_shape=jax.ShapeDtypeStruct((CELLS, EQ, LANES),...]
where the time goes in v2:
time: 53.7 us; the launch traced here: 53.5 us
  Pallas kernels  52 us (97%)
  local copies, waits for them, and re-layouts  1.47 us (3%)
    pallas_call x1, Pallas kernels, on_device(): pl.pallas_call(kernel, out_shape=jax.ShapeDtypeStruct((CELLS, EQ, LANES),...  52 us
    unnamed x1, local copies, waits for them, and re-layouts  1.47 us

profile of v2, /device:TPU:8, one launch (start us, length us, event | category | flops | bytes accessed | tf_op | source)
XLA Modules:
  0.0 53.5 jit_solution(12541372475947506964)
XLA Ops:
  0.0 52.0 %shard_map.82 = f32[8,16,128]{2,1,0:T(8,128)} custom-call(f32[8,16,128]{2,1,0:T(8,128)} %rhs_hbm.1, bf16[8,16,16,128]{3,2,1,0:T(8,128)(2,1)} %pivot_hbm.1, bf16[8,16,16,128]{3,2,1,0:T(8,128)(2,1)} %lower_hbm.1, bf16[8,16,16,128]{3,2,1,0:T(8,128)(2,1)} %upper_hbm.1, bf16[8,16,16,128]{3,2,1,0:T(8,128)(2,1)} %west_hbm.1, bf16[8,16,16,128]{3,2,1,0:T(8,128)(2,1)} %east_hbm.1, ...), custom_call_target="tpu_custom_call" | custom-call | tf_op jit(solution)/shard_map/pallas_call | solution.py:486
  52.0 1.5 %copy.10 = f32[8,16,128]{2,1,0:T(8,128)} copy(f32[8,16,128]{2,1,0:T(8,128)} %shard_map.82) | data formatting | bytes 131072

commit v3 on v2

--- a/solution.py
+++ b/solution.py
@@ -44,8 +44,7 @@
 
 
 def block_product(out, out_base, left, left_base, right, right_base, add=None, add_base=0):
-    def some_columns(step, carry):
-        first = pl.multiple_of(step * (4 * EQ), 4 * EQ)
+    for first in range(0, BLOCK, 4 * EQ):
         sums = [None] * 4
         if add is not None:
             sums = [add[rows(add_base + first + EQ * m, EQ), :] for m in range(4)]
@@ -56,9 +55,6 @@
                 sums[m] = term if sums[m] is None else sums[m] + term
         for m in range(4):
             out[rows(out_base + first + EQ * m, EQ), :] = sums[m]
-        return carry
-
-    lax.fori_loop(0, 4, some_columns, 0)
 
 
 def swap_four(values, slot, width):
@@ -73,8 +69,8 @@
 
 
 def kernel(
-    rhs_hbm, pivot_hbm, lower_hbm, upper_hbm, west_hbm, east_hbm, mask_in, codes, out,
-    rhs, pivot_in, lower_in, upper_in, west_in, east_in,
+    rhs_hbm, pivot_hbm, lower_hbm, upper_hbm, west_hbm, east_hbm, mask_hbm, codes_hbm, out,
+    rhs, pivot_in, lower_in, upper_in, west_in, east_in, mask_in, codes,
     temp, mask_cols, pivot, lower, upper, west, east, c_maps, d_maps, b_maps, others,
     f_rows, q_rows, r_rows, uw_rows, ue_rows, s_rows, ab_rows,
     q_all, r_all, a_all, b_all,
@@ -102,6 +98,8 @@
                 (rhs_hbm, rhs),
                 (west_hbm, west_in),
                 (east_hbm, east_in),
+                (mask_hbm, mask_in),
+                (codes_hbm, codes),
             ]
         )
     ]
@@ -114,19 +112,20 @@
     for other in (next_stream, last_stream):
         pl.semaphore_signal(barrier, inc=1, device_id={"stream": other}, device_id_type=MESH)
 
-    def by_columns(load, source, target, scale=None):
-        load.wait()
-
+    def column_cell(j, source, target, scale=None):
+        base = pl.multiple_of(j * BLOCK, BLOCK)
+        for c in range(EQ):
+            temp[rows(base + EQ * c, EQ), :] = source[j, c].astype(F32)
+        factor = None if scale is None else scale(j)
+        for k in range(EQ):
+            column = temp[pl.ds(base + k, EQ, stride=EQ), :]
+            if factor is not None:
+                column = column * (mask_cols[EQ * k : EQ * k + EQ, :] * factor)
+            target[rows(base + EQ * k, EQ), :] = column
+
+    def by_columns(source, target, scale=None):
         def one_cell(j, carry):
-            base = pl.multiple_of(j * BLOCK, BLOCK)
-            for c in range(EQ):
-                temp[rows(base + EQ * c, EQ), :] = source[j, c].astype(F32)
-            factor = None if scale is None else scale(j)
-            for k in range(EQ):
-                column = temp[pl.ds(base + k, EQ, stride=EQ), :]
-                if factor is not None:
-                    column = column * (mask_cols[EQ * k : EQ * k + EQ, :] * factor)
-                target[rows(base + EQ * k, EQ), :] = column
+            column_cell(j, source, target, scale)
             return carry
 
         lax.fori_loop(0, CELLS, one_cell, 0)
@@ -179,19 +178,24 @@
                 others[rows(at, EQ), :] = pltpu.roll(value, shifts[m], 1)
         return carry
 
-    by_columns(loads[0], lower_in, lower)
+    loads[0].wait()
+    by_columns(lower_in, lower)
+    loads[1].wait()
+    column_cell(0, upper_in, upper)
     c_maps[0:BLOCK, :] = lower[0:BLOCK, :]
 
     def c_cell(j, carry):
         base = pl.multiple_of(j * BLOCK, BLOCK)
         block_product(c_maps, base, lower, base, c_maps, base - BLOCK)
+        column_cell(j, upper_in, upper)
         return carry
 
     lax.fori_loop(1, CELLS, c_cell, 0)
     pl.semaphore_wait(barrier, len(peers) + 2)
     send_map(0, c_maps, (CELLS - 1) * BLOCK)
 
-    by_columns(loads[1], upper_in, upper)
+    loads[2].wait()
+    column_cell(0, pivot_in, pivot)
     d_maps[(CELLS - 1) * BLOCK : CELLS * BLOCK, :] = upper[(CELLS - 1) * BLOCK : CELLS * BLOCK, :]
     final = (CELLS - 1) * BLOCK
     b_maps[final : final + BLOCK, :] = c_maps[final : final + BLOCK, :]
@@ -199,18 +203,11 @@
     def b_cell(step, carry):
         base = pl.multiple_of((CELLS - 1 - step) * BLOCK, BLOCK)
         block_product(b_maps, base, upper, base, b_maps, base + BLOCK, c_maps, base)
+        column_cell(step, pivot_in, pivot)
         return carry
 
     lax.fori_loop(1, CELLS, b_cell, 0)
     send_map(1, b_maps, 0)
-
-    def d_cell(step, carry):
-        base = pl.multiple_of((CELLS - 1 - step) * BLOCK, BLOCK)
-        block_product(d_maps, base, upper, base, d_maps, base + BLOCK)
-        return carry
-
-    lax.fori_loop(1, CELLS, d_cell, 0)
-    send_map(2, d_maps, 0)
 
     def forward_cell(j):
         block = jnp.minimum(j, CELLS - 1)
@@ -332,7 +329,6 @@
         for v, value in enumerate(swap_four(values, high_slot, 32)):
             ab_rows[8 * v : 8 * v + 8, :] = value
 
-    by_columns(loads[2], pivot_in, pivot)
     loads[3].wait()
     for j in range(CELLS):
         s_rows[EQ * j : EQ * j + EQ, :] = rhs[j]
@@ -349,6 +345,17 @@
     down_chain()
     send_up()
 
+    def d_cell(step, carry):
+        base = pl.multiple_of((CELLS - 1 - step) * BLOCK, BLOCK)
+        block_product(d_maps, base, upper, base, d_maps, base + BLOCK)
+        return carry
+
+    lax.fori_loop(1, CELLS, d_cell, 0)
+    send_map(2, d_maps, 0)
+
+    loads[6].wait()
+    loads[7].wait()
+
     for k in range(EQ):
         column = mask_in[:, k : k + 1].astype(F32)
         mask_cols[EQ * k : EQ * k + EQ, :] = jnp.broadcast_to(column, (EQ, LANES))
@@ -361,11 +368,12 @@
         code = codes[rows(j, 1), :]
         return jnp.where((code == 0) | (code == 2), 1.0, 0.0).astype(F32)
 
-    by_columns(loads[4], west_in, west, west_on)
-    by_columns(loads[5], east_in, east, east_on)
+    loads[4].wait()
+    by_columns(west_in, west, west_on)
+    loads[5].wait()
+    by_columns(east_in, east, east_on)
     a_all[0:EQ, :] = jnp.zeros((EQ, LANES), F32)
     b_all[(WALL - 1) * EQ : WALL * EQ, :] = jnp.zeros((EQ, LANES), F32)
-    lax.fori_loop(0, 3, take_map, 0)
 
     def halo_copy(sweep, side, other):
         return pltpu.make_async_remote_copy(
@@ -385,33 +393,33 @@
             rhs[block] - times(west, base, uw_rows, at) - times(east, base, ue_rows, at)
         )
 
+    maps_b, maps_d = WALL * BLOCK, 2 * WALL * BLOCK
+
+    def rise():
+        a_all[EQ : 2 * EQ, :] = q_all[0:EQ, :]
+        for i in range(1, WALL):
+            part = slice(EQ * i, EQ * i + EQ)
+            if i < WALL - 1:
+                a_all[EQ * i + EQ : EQ * i + 2 * EQ, :] = q_all[part, :] + times(
+                    others, BLOCK * i, a_all, EQ * i
+                )
+            total = r_all[part, :] + times(others, maps_b + BLOCK * i, a_all, EQ * i)
+            if i < WALL - 1:
+                r_all[part, :] = total
+            else:
+                b_all[EQ * i - EQ : EQ * i, :] = total
+
+    lax.fori_loop(0, 2, take_map, 0)
+    take_up()
+    rise()
+    take_map(2, 0)
+
     def one_sweep(sweep, carry):
-        take_up()
-
-        a_all[EQ : 2 * EQ, :] = q_all[0:EQ, :]
-        maps_b, maps_d = WALL * BLOCK, 2 * WALL * BLOCK
-
-        def rise(i, carry):
-            at = pl.multiple_of(i * EQ, EQ)
-            base = pl.multiple_of(i * BLOCK, BLOCK)
-            a_all[rows(at + EQ, EQ), :] = q_all[rows(at, EQ), :] + times(others, base, a_all, at)
-            r_all[rows(at, EQ), :] = r_all[rows(at, EQ), :] + times(others, maps_b + base, a_all, at)
-            return carry
-
-        lax.fori_loop(1, WALL - 1, rise, 0)
-        last = (WALL - 1) * EQ
-        b_all[last - EQ : last, :] = r_all[last : last + EQ, :] + times(
-            others, maps_b + (WALL - 1) * BLOCK, a_all, last
-        )
-
-        def fall(step, carry):
+        for step in range(1, WALL - 1):
             i = WALL - 1 - step
-            at = pl.multiple_of(i * EQ, EQ)
-            base = pl.multiple_of(i * BLOCK, BLOCK)
-            b_all[rows(at - EQ, EQ), :] = r_all[rows(at, EQ), :] + times(others, maps_d + base, b_all, at)
-            return carry
-
-        lax.fori_loop(1, WALL - 1, fall, 0)
+            b_all[EQ * i - EQ : EQ * i, :] = r_all[EQ * i : EQ * i + EQ, :] + times(
+                others, maps_d + BLOCK * i, b_all, EQ * i
+            )
         send_back()
         take_back()
 
@@ -468,6 +476,8 @@
             lax.fori_loop(1, CELLS, next_up, 0)
             down_chain()
             send_up()
+            take_up()
+            rise()
 
         return carry
 
@@ -486,11 +496,11 @@
     return pl.pallas_call(
         kernel,
         out_shape=jax.ShapeDtypeStruct((CELLS, EQ, LANES), F32),
-        in_specs=[pl.BlockSpec(memory_space=pl.ANY)] * 6
-        + [pl.BlockSpec(memory_space=pltpu.VMEM)] * 2,
+        in_specs=[pl.BlockSpec(memory_space=pltpu.HBM)] * 8,
         out_specs=pl.BlockSpec(memory_space=pltpu.VMEM),
         scratch_shapes=[
             pltpu.VMEM((CELLS, EQ, LANES), F32), narrow, narrow, narrow, narrow, narrow,
+            pltpu.VMEM((EQ, EQ), jnp.int32), pltpu.VMEM((CELLS, LANES), jnp.int32),
             big, block, big, big, big, big, big, big, big, big,
             pltpu.VMEM((3 * WALL * BLOCK, LANES), F32),
             padded, vectors, vectors, vectors, vectors, padded, pair,
@@ -500,7 +510,7 @@
             pltpu.VMEM((SIDE, 8, LANES), F32), tiles, tiles, tiles,
             pltpu.VMEM((SWEEPS - 1, 2, EQ, LANES), F32),
             pltpu.VMEM((SWEEPS - 1, 2, EQ, LANES), F32),
-            pltpu.SemaphoreType.DMA((6,)),
+            pltpu.SemaphoreType.DMA((8,)),
             pltpu.SemaphoreType.DMA((3, WALL)),
             pltpu.SemaphoreType.DMA((3, WALL)),
             pltpu.SemaphoreType.DMA((2, WALL)),

time: 53.7 us -> 52.1 us (0.970)
  Pallas kernels: 52 us -> 50.4 us
    pallas_call x1, Pallas kernels: 52 us -> 50.4 us  [on_device(): pl.pallas_call(kernel, out_shape=jax.ShapeDtypeStruct((CELLS, EQ, LANES),...]
where the time goes in v3:
time: 52.1 us; the launch traced here: 51.9 us
  Pallas kernels  50.4 us (97%)
  local copies, waits for them, and re-layouts  1.47 us (3%)
    pallas_call x1, Pallas kernels, on_device(): pl.pallas_call(kernel, out_shape=jax.ShapeDtypeStruct((CELLS, EQ, LANES),...  50.4 us
    unnamed x1, local copies, waits for them, and re-layouts  1.47 us

profile of v3, /device:TPU:8, one launch (start us, length us, event | category | flops | bytes accessed | tf_op | source)
XLA Modules:
  0.0 51.9 jit_solution(3510343477514793309)
XLA Ops:
  0.0 50.4 %shard_map.82 = f32[8,16,128]{2,1,0:T(8,128)} custom-call(f32[8,16,128]{2,1,0:T(8,128)} %rhs_hbm.1, bf16[8,16,16,128]{3,2,1,0:T(8,128)(2,1)} %pivot_hbm.1, bf16[8,16,16,128]{3,2,1,0:T(8,128)(2,1)} %lower_hbm.1, bf16[8,16,16,128]{3,2,1,0:T(8,128)(2,1)} %upper_hbm.1, bf16[8,16,16,128]{3,2,1,0:T(8,128)(2,1)} %west_hbm.1, bf16[8,16,16,128]{3,2,1,0:T(8,128)(2,1)} %east_hbm.1, ...), custom_call_target="tpu_custom_call" | custom-call | tf_op jit(solution)/shard_map/pallas_call | solution.py:496
  50.5 1.5 %copy.10 = f32[8,16,128]{2,1,0:T(8,128)} copy(f32[8,16,128]{2,1,0:T(8,128)} %shard_map.82) | data formatting | bytes 131072

commit v4 on v3

--- a/solution.py
+++ b/solution.py
@@ -75,7 +75,9 @@
     f_rows, q_rows, r_rows, uw_rows, ue_rows, s_rows, ab_rows,
     q_all, r_all, a_all, b_all,
     map_out, map_in, up_out, up_in, back_out, back_in, halo_out, halo_in,
+    edge_out, edge_in, b_edge, d_edge, ghost_in, ghost_ab,
     load_sem, map_send, map_recv, vec_send, vec_recv, halo_send, halo_recv,
+    edge_send, edge_recv, ghost_send, ghost_recv, ready,
 ):
     me = lax.axis_index("wall")
     stream = lax.axis_index("stream")
@@ -192,6 +194,13 @@
 
     lax.fori_loop(1, CELLS, c_cell, 0)
     pl.semaphore_wait(barrier, len(peers) + 2)
+
+    for owner in (WALL - 1, 0):
+
+        @pl.when(me != owner)
+        def _():
+            pl.semaphore_signal(ready, inc=1, device_id={"wall": owner}, device_id_type=MESH)
+
     send_map(0, c_maps, (CELLS - 1) * BLOCK)
 
     loads[2].wait()
@@ -299,7 +308,67 @@
             r_all[EQ * i : EQ * i + 8, :] = pltpu.roll(tile, LANES - 64, 1)
             r_all[EQ * i + 8 : EQ * i + 16, :] = pltpu.roll(tile, LANES - 96, 1)
 
-    def send_back():
+    def ghost_copy(sweep, side, i):
+        return pltpu.make_async_remote_copy(
+            src_ref=back_out.at[i],
+            dst_ref=ghost_in.at[sweep, side],
+            send_sem=ghost_send.at[sweep, i],
+            recv_sem=ghost_recv.at[sweep, side],
+            device_id={"wall": i, "stream": last_stream if side else next_stream},
+            device_id_type=MESH,
+        )
+
+    def on_ghosts(sweep, act):
+        for side, owner in ((0, WALL - 1), (1, 0)):
+
+            @pl.when((sweep < SWEEPS - 1) & (me == owner))
+            def _():
+                for i in range(WALL):
+                    act(ghost_copy(sweep, side, i))
+
+    def pack_edges(values):
+        to_next, to_last = None, None
+        for j, value in enumerate(values):
+            high, low = pltpu.roll(value, j + 1, 1), pltpu.roll(value, 8 + j, 1)
+            to_next = high if j == 0 else jnp.where(lane16 == j, high, to_next)
+            to_last = low if j == 0 else jnp.where(lane16 == 8 + j, low, to_last)
+        return to_next, to_last
+
+    def edge_copy(side, other):
+        return pltpu.make_async_remote_copy(
+            src_ref=edge_out.at[side],
+            dst_ref=edge_in.at[side],
+            send_sem=edge_send.at[side],
+            recv_sem=edge_recv.at[side],
+            device_id={"stream": other},
+            device_id_type=MESH,
+        )
+
+    def send_edge_maps():
+        def some_columns(step, carry):
+            for m in range(8):
+                at = pl.multiple_of(step * (8 * EQ) + EQ * m, EQ)
+                for which, maps in enumerate((b_maps, d_maps)):
+                    pair = pack_edges([maps[rows(BLOCK * j + at, EQ), :] for j in range(CELLS)])
+                    for side in range(2):
+                        edge_out[side, which, rows(at, EQ), :] = pair[side]
+            return carry
+
+        lax.fori_loop(0, 2, some_columns, 0)
+        edge_copy(0, next_stream).start()
+        edge_copy(1, last_stream).start()
+
+    def take_edge_maps():
+        edge_copy(0, next_stream).wait()
+        edge_copy(1, last_stream).wait()
+        for m in range(EQ):
+            part = slice(EQ * m, EQ * m + EQ)
+            for which, maps in enumerate((b_edge, d_edge)):
+                maps[part, :] = jnp.where(
+                    lane16 < 8, edge_in[0, which, part, :], edge_in[1, which, part, :]
+                )
+
+    def send_back(sweep):
         for i in range(WALL):
             tile = a_all[EQ * i : EQ * i + 8, :]
             for v, piece in enumerate(
@@ -311,6 +380,12 @@
             ):
                 tile = jnp.where(high_slot == v + 1, pltpu.roll(piece, 32 * (v + 1), 1), tile)
             back_out[i] = tile
+
+        @pl.when((sweep == 0) & (me % (WALL - 1) == 0))
+        def _():
+            pl.semaphore_wait(ready, WALL - 1)
+
+        on_ghosts(sweep, lambda copy: copy.start())
         for peer in peers:
             back_copy(peer).start()
         back_in[me] = back_out[me]
@@ -368,10 +443,7 @@
         code = codes[rows(j, 1), :]
         return jnp.where((code == 0) | (code == 2), 1.0, 0.0).astype(F32)
 
-    loads[4].wait()
-    by_columns(west_in, west, west_on)
-    loads[5].wait()
-    by_columns(east_in, east, east_on)
+    send_edge_maps()
     a_all[0:EQ, :] = jnp.zeros((EQ, LANES), F32)
     b_all[(WALL - 1) * EQ : WALL * EQ, :] = jnp.zeros((EQ, LANES), F32)
 
@@ -420,8 +492,25 @@
             b_all[EQ * i - EQ : EQ * i, :] = r_all[EQ * i : EQ * i + EQ, :] + times(
                 others, maps_d + BLOCK * i, b_all, EQ * i
             )
-        send_back()
+        send_back(sweep)
+
+        @pl.when(sweep < SWEEPS - 1)
+        def _():
+            pair = pack_edges([r_rows[EQ * j : EQ * j + EQ, :] for j in range(CELLS)])
+            for side, other in ((0, next_stream), (1, last_stream)):
+                halo_out[sweep, side] = pair[side]
+                halo_copy(sweep, side, other).start()
+
+        @pl.when(sweep == 0)
+        def _():
+            loads[4].wait()
+            by_columns(west_in, west, west_on)
+            loads[5].wait()
+            by_columns(east_in, east, east_on)
+            take_edge_maps()
+
         take_back()
+        on_ghosts(sweep, lambda copy: copy.wait_send())
 
         def update_cell(j, carry):
             base = pl.multiple_of(j * BLOCK, BLOCK)
@@ -437,27 +526,39 @@
 
         @pl.when(sweep < SWEEPS - 1)
         def _():
-            to_east = pltpu.roll(out[0], 1, 1)
-            to_west = out[0]
-            for j in range(1, CELLS):
-                to_east = jnp.where(lane16 == j, pltpu.roll(out[j], j + 1, 1), to_east)
-                to_west = jnp.where(lane16 == j, pltpu.roll(out[j], j, 1), to_west)
-            halo_out[sweep, 0] = to_east
-            halo_out[sweep, 1] = to_west
-            halo_copy(sweep, 0, next_stream).start()
-            halo_copy(sweep, 1, last_stream).start()
             for j in range(CELLS):
                 uw_rows[EQ * j : EQ * j + EQ, :] = pltpu.roll(out[j], 1, 1)
                 ue_rows[EQ * j : EQ * j + EQ, :] = pltpu.roll(out[j], LANES - 1, 1)
-            halo_copy(sweep, 0, next_stream).wait()
-            halo_copy(sweep, 1, last_stream).wait()
-            from_west = jnp.where(stream == 0, 0.0, halo_in[sweep, 0])
-            from_east = jnp.where(stream == streams - 1, 0.0, halo_in[sweep, 1])
+            for side, other in ((0, next_stream), (1, last_stream)):
+                halo_copy(sweep, side, other).wait()
+            for side in range(2):
+                pltpu.make_async_remote_copy(
+                    src_ref=back_out.at[0],
+                    dst_ref=ghost_in.at[sweep, side],
+                    send_sem=ghost_send.at[sweep, 0],
+                    recv_sem=ghost_recv.at[sweep, side],
+                    device_id={"stream": next_stream},
+                    device_id_type=MESH,
+                ).wait_recv()
+            from_west, from_east = ghost_in[sweep, 0], ghost_in[sweep, 1]
+            for v in range(SIDE):
+                ghost_ab[8 * v : 8 * v + 8, :] = jnp.where(
+                    lane < 8,
+                    jnp.broadcast_to(from_west[:, 32 * v + 31 : 32 * v + 32], (8, LANES)),
+                    jnp.broadcast_to(from_east[:, 32 * v : 32 * v + 1], (8, LANES)),
+                )
+            ghosts = (
+                jnp.where(lane16 < 8, halo_in[sweep, 0], halo_in[sweep, 1])
+                + times(b_edge, 0, ghost_ab, 0)
+                + times(d_edge, 0, ghost_ab, EQ)
+            )
+            west_ghosts = jnp.where(stream == 0, 0.0, ghosts)
+            east_ghosts = jnp.where(stream == streams - 1, 0.0, ghosts)
             for j in range(CELLS):
                 part = slice(EQ * j, EQ * j + EQ)
-                ghost = pltpu.roll(from_west, LANES - j, 1) if j else from_west
+                ghost = pltpu.roll(west_ghosts, LANES - j, 1) if j else west_ghosts
                 uw_rows[part, :] = jnp.where(lane16 == 0, ghost, uw_rows[part, :])
-                ghost = pltpu.roll(from_east, LANES - 1 - j, 1)
+                ghost = pltpu.roll(east_ghosts, LANES - 9 - j, 1)
                 ue_rows[part, :] = jnp.where(lane16 == LANES - 1, ghost, ue_rows[part, :])
 
             source_cell(0)
@@ -510,6 +611,11 @@
             pltpu.VMEM((SIDE, 8, LANES), F32), tiles, tiles, tiles,
             pltpu.VMEM((SWEEPS - 1, 2, EQ, LANES), F32),
             pltpu.VMEM((SWEEPS - 1, 2, EQ, LANES), F32),
+            pltpu.VMEM((2, 2, BLOCK, LANES), F32),
+            pltpu.VMEM((2, 2, BLOCK, LANES), F32),
+            block, block,
+            pltpu.VMEM((SWEEPS - 1, 2, 8, LANES), F32),
+            pair,
             pltpu.SemaphoreType.DMA((8,)),
             pltpu.SemaphoreType.DMA((3, WALL)),
             pltpu.SemaphoreType.DMA((3, WALL)),
@@ -517,6 +623,11 @@
             pltpu.SemaphoreType.DMA((2, WALL)),
             pltpu.SemaphoreType.DMA((SWEEPS - 1, 2)),
             pltpu.SemaphoreType.DMA((SWEEPS - 1, 2)),
+            pltpu.SemaphoreType.DMA((2,)),
+            pltpu.SemaphoreType.DMA((2,)),
+            pltpu.SemaphoreType.DMA((SWEEPS - 1, WALL)),
+            pltpu.SemaphoreType.DMA((SWEEPS - 1, 2)),
+            pltpu.SemaphoreType.REGULAR,
         ],
         compiler_params=pltpu.CompilerParams(collective_id=0, has_side_effects=True),
     )(*arrays)

time: 52.1 us -> 50.2 us (0.964)
  Pallas kernels: 50.4 us -> 48.5 us
    pallas_call x1, Pallas kernels: 50.4 us -> 48.5 us  [on_device(): pl.pallas_call(kernel, out_shape=jax.ShapeDtypeStruct((CELLS, EQ, LANES),...]
where the time goes in v4:
time: 50.2 us; the launch traced here: 50 us
  Pallas kernels  48.5 us (97%)
  local copies, waits for them, and re-layouts  1.47 us (3%)
    pallas_call x1, Pallas kernels, on_device(): pl.pallas_call(kernel, out_shape=jax.ShapeDtypeStruct((CELLS, EQ, LANES),...  48.5 us
    unnamed x1, local copies, waits for them, and re-layouts  1.47 us

profile of v4, /device:TPU:8, one launch (start us, length us, event | category | flops | bytes accessed | tf_op | source)
XLA Modules:
  0.0 50.0 jit_solution(5086925027910923731)
XLA Ops:
  0.0 48.5 %shard_map.82 = f32[8,16,128]{2,1,0:T(8,128)} custom-call(f32[8,16,128]{2,1,0:T(8,128)} %rhs_hbm.1, bf16[8,16,16,128]{3,2,1,0:T(8,128)(2,1)} %pivot_hbm.1, bf16[8,16,16,128]{3,2,1,0:T(8,128)(2,1)} %lower_hbm.1, bf16[8,16,16,128]{3,2,1,0:T(8,128)(2,1)} %upper_hbm.1, bf16[8,16,16,128]{3,2,1,0:T(8,128)(2,1)} %west_hbm.1, bf16[8,16,16,128]{3,2,1,0:T(8,128)(2,1)} %east_hbm.1, ...), custom_call_target="tpu_custom_call" | custom-call | tf_op jit(solution)/shard_map/pallas_call | solution.py:597
  48.5 1.5 %copy.10 = f32[8,16,128]{2,1,0:T(8,128)} copy(f32[8,16,128]{2,1,0:T(8,128)} %shard_map.82) | data formatting | bytes 131072

commit v5 on v4

--- a/solution.py
+++ b/solution.py
@@ -86,6 +86,8 @@
     peers = [((my_y + dy) % SIDE) * SIDE + (my_x + dx) % SIDE for dy, dx in OFFSETS]
     next_stream = lax.rem(stream + 1, streams)
     last_stream = lax.rem(stream + streams - 1, streams)
+    sends = (stream < streams - 1, stream > 0)
+    takes = (stream > 0, stream < streams - 1)
     lane = lax.broadcasted_iota(jnp.int32, (8, LANES), 1)
     lane16 = lax.broadcasted_iota(jnp.int32, (EQ, LANES), 1)
     high_slot, low_slot = lane // 32, (lane // 8) % SIDE
@@ -321,7 +323,7 @@
     def on_ghosts(sweep, act):
         for side, owner in ((0, WALL - 1), (1, 0)):
 
-            @pl.when((sweep < SWEEPS - 1) & (me == owner))
+            @pl.when((sweep < SWEEPS - 1) & (me == owner) & sends[side])
             def _():
                 for i in range(WALL):
                     act(ghost_copy(sweep, side, i))
@@ -355,12 +357,13 @@
             return carry
 
         lax.fori_loop(0, 2, some_columns, 0)
-        edge_copy(0, next_stream).start()
-        edge_copy(1, last_stream).start()
+        for side, other in ((0, next_stream), (1, last_stream)):
+            pl.when(sends[side])(edge_copy(side, other).start)
 
     def take_edge_maps():
-        edge_copy(0, next_stream).wait()
-        edge_copy(1, last_stream).wait()
+        for side, other in ((0, next_stream), (1, last_stream)):
+            pl.when(sends[side])(edge_copy(side, other).wait_send)
+            pl.when(takes[side])(edge_copy(side, other).wait_recv)
         for m in range(EQ):
             part = slice(EQ * m, EQ * m + EQ)
             for which, maps in enumerate((b_edge, d_edge)):
@@ -499,7 +502,7 @@
             pair = pack_edges([r_rows[EQ * j : EQ * j + EQ, :] for j in range(CELLS)])
             for side, other in ((0, next_stream), (1, last_stream)):
                 halo_out[sweep, side] = pair[side]
-                halo_copy(sweep, side, other).start()
+                pl.when(sends[side])(halo_copy(sweep, side, other).start)
 
         @pl.when(sweep == 0)
         def _():
@@ -530,16 +533,18 @@
                 uw_rows[EQ * j : EQ * j + EQ, :] = pltpu.roll(out[j], 1, 1)
                 ue_rows[EQ * j : EQ * j + EQ, :] = pltpu.roll(out[j], LANES - 1, 1)
             for side, other in ((0, next_stream), (1, last_stream)):
-                halo_copy(sweep, side, other).wait()
+                pl.when(sends[side])(halo_copy(sweep, side, other).wait_send)
+                pl.when(takes[side])(halo_copy(sweep, side, other).wait_recv)
             for side in range(2):
-                pltpu.make_async_remote_copy(
+                arrival = pltpu.make_async_remote_copy(
                     src_ref=back_out.at[0],
                     dst_ref=ghost_in.at[sweep, side],
                     send_sem=ghost_send.at[sweep, 0],
                     recv_sem=ghost_recv.at[sweep, side],
                     device_id={"stream": next_stream},
                     device_id_type=MESH,
-                ).wait_recv()
+                )
+                pl.when(takes[side])(arrival.wait_recv)
             from_west, from_east = ghost_in[sweep, 0], ghost_in[sweep, 1]
             for v in range(SIDE):
                 ghost_ab[8 * v : 8 * v + 8, :] = jnp.where(

time: 50.2 us -> 48.2 us (0.960)
  Pallas kernels: 48.5 us -> 46.5 us
    pallas_call x1, Pallas kernels: 48.5 us -> 46.5 us  [on_device(): pl.pallas_call(kernel, out_shape=jax.ShapeDtypeStruct((CELLS, EQ, LANES),...]
where the time goes in v5:
time: 48.2 us; the launch traced here: 48 us
  Pallas kernels  46.5 us (96%)
  local copies, waits for them, and re-layouts  1.47 us (3%)
    pallas_call x1, Pallas kernels, on_device(): pl.pallas_call(kernel, out_shape=jax.ShapeDtypeStruct((CELLS, EQ, LANES),...  46.5 us
    unnamed x1, local copies, waits for them, and re-layouts  1.47 us

profile of v5, /device:TPU:8, one launch (start us, length us, event | category | flops | bytes accessed | tf_op | source)
XLA Modules:
  0.0 48.0 jit_solution(1894326014079361898)
XLA Ops:
  0.0 46.5 %shard_map.82 = f32[8,16,128]{2,1,0:T(8,128)} custom-call(f32[8,16,128]{2,1,0:T(8,128)} %rhs_hbm.1, bf16[8,16,16,128]{3,2,1,0:T(8,128)(2,1)} %pivot_hbm.1, bf16[8,16,16,128]{3,2,1,0:T(8,128)(2,1)} %lower_hbm.1, bf16[8,16,16,128]{3,2,1,0:T(8,128)(2,1)} %upper_hbm.1, bf16[8,16,16,128]{3,2,1,0:T(8,128)(2,1)} %west_hbm.1, bf16[8,16,16,128]{3,2,1,0:T(8,128)(2,1)} %east_hbm.1, ...), custom_call_target="tpu_custom_call" | custom-call | tf_op jit(solution)/shard_map/pallas_call | solution.py:602
  46.5 1.5 %copy.10 = f32[8,16,128]{2,1,0:T(8,128)} copy(f32[8,16,128]{2,1,0:T(8,128)} %shard_map.82) | data formatting | bytes 131072
